TPU v7x, 128 devices: a whole 4x4x4 slice. The times are simulated.
128 devices in a mesh: contour: 4 (over x), clus: 32 (over y, z, core).
Axes of the slice: x: 4, y: 4, z: 4, core: 2. Of those that a mesh axis runs over, the one named last changes fastest.
Arguments:
- probes: float32 [256, 2, 16, 128], P('clus'), may hold values from -18 to 18
- near_blocks: bfloat16 [1024, 27, 2, 128, 128], P(('contour', 'clus')), parts along dimension 0
- near_list: int32 [256, 27], P('clus'), may hold values from 0 to 255, as said below
- near_count: int32 [256], P('clus'), may hold values from 1 to 27
- cluster_rows: int32 [256], P('clus'), may hold values from 64 to 128
- row_basis: bfloat16 [1024, 2, 32, 128], P(('contour', 'clus')), parts along dimension 0, may hold values from -1 to 1
- col_basis: bfloat16 [1024, 2, 32, 128], P(('contour', 'clus')), parts along dimension 0, may hold values from -0.5 to 0.5
- far_list: int32 [256, 32], P('clus'), may hold values from 0 to 255, as said below
- far_coupling: float32 [1024, 32, 2, 32, 32], P(('contour', 'clus')), parts along dimension 0, may hold values from -0.375 to 0.375
- weight: float32 [8], P('contour'), parts along dimension 0, may hold values from -6 to 6
Outputs:
- solution: float32 [1024, 2, 16, 128], P(('contour', 'clus')), parts along dimension 0
- moment: float32 [8, 16, 16], P('contour'), parts along dimension 0
- arnoldi: float32 [16, 16], P('contour'), parts along dimension 0
There are 4 independent parts, one for each index of `contour`. A program takes and returns all parts, laid end to end along the dimension named above; an argument that names none is the same for every part. Nothing has to cross between parts.
Inputs may be any that keep to these rules, and one draw needn't show every extreme that they name: near_list[i, 0] = i; every entry lies within 8 clusters of i. `far_list`: every entry j of cluster i's list has min(|j - i|, 256 - |j - i|) > 8, so no far slot names a cluster of i's near list.
All inputs are finite; a program needn't handle non-finite values.
Results may differ from a plain program's by a relative error of at most 0.0019.
Values may be sent and summed in bfloat16 or wider, within the bound.
No kernel may reach another device: no remote copies, remote signals or barrier semaphores. Data moves between devices by JAX's collectives and lax.ppermute only.
A program may use at most 128 MiB of HBM per device.

v0:
```python
import functools

import jax
import jax.numpy as jnp
from jax import lax
from jax.experimental import pallas as pl
from jax.experimental.pallas import tpu as pltpu
from jax.sharding import PartitionSpec as P


F32 = jnp.float32
BF16 = jnp.bfloat16
OWN = 8
RANK = 32
PROBES = 16
FMAX = 32
KMAX = 27
NEAR_SPLIT = (3, 3, 2)
STAT = 64
PAY = 80
VMEM = pl.BlockSpec(memory_space=pltpu.VMEM)
SMEM = pl.BlockSpec(memory_space=pltpu.SMEM)


def dot_nt(left, right):
    return lax.dot_general(left, right, (((1,), (1,)), ((), ())), preferred_element_type=F32)


def dot_nn(left, right):
    return lax.dot_general(left, right, (((1,), (0,)), ((), ())), preferred_element_type=F32)


def dot_tn(left, right):
    return lax.dot_general(left, right, (((0,), (0,)), ((), ())), preferred_element_type=F32)


def lanes(rows):
    return lax.broadcasted_iota(jnp.int32, (rows, 128), 1)


def paired(field):
    re, im = field[:PROBES], field[PROBES:]
    return jnp.concatenate(
        [jnp.concatenate([re, -im], axis=1), jnp.concatenate([im, re], axis=1)], axis=0
    )


def high_low(value):
    high = value.astype(BF16)
    return high, (value - high.astype(F32)).astype(BF16)


def coefficients(pair, basis):
    both = jnp.concatenate([basis[0], basis[1]], axis=1)
    return dot_nt(both, jnp.concatenate([pair] * 4, axis=0))


def side_by_side(wide):
    block = lanes(RANK) // RANK
    return jnp.where(
        block < 2,
        jnp.where(block == 0, wide[0], wide[1]),
        jnp.where(block == 2, wide[2], wide[3]),
    )


def three_way(column, at):
    lane = lanes(PROBES)
    value = jnp.broadcast_to(column, (PROBES, 128))
    high = value.astype(BF16).astype(F32)
    rest = value - high
    mid = rest.astype(BF16).astype(F32)
    low = rest - mid
    zero = jnp.zeros((PROBES, 128), F32)
    return jnp.where(
        lane == at, high, jnp.where(lane == 32 + at, mid, jnp.where(lane == 64 + at, low, zero))
    )


def column_of(tile, *at):
    lane = lanes(PROBES)
    keep = lane == at[0]
    for a in at[1:]:
        keep = keep | (lane == a)
    return jnp.sum(jnp.where(keep, tile, 0.0), axis=1, keepdims=True)


def gathered_stat(mine, other):
    total = jnp.zeros((PROBES, 128), F32)
    for ref in (mine, other):
        for slot in range(16):
            total = total + ref[slot, STAT:PAY].astype(F32)
    return total


def lane_sum(value):
    return jnp.sum(value, axis=1, keepdims=True)


def twice(column):
    return jnp.concatenate([column, column], axis=0)


def front_kernel(rows, near_list, far_list, probes, col_basis, base, pay, near_at, far_at):
    me = lax.axis_index("clus")
    local = near_list[...] - me * OWN
    flip = (me & 1) * OWN
    near_at[...] = jnp.where(
        local < 0, local + 3 * OWN - flip, jnp.where(local < OWN, local, local + flip)
    )
    far = far_list[...]
    owner = far >> 3
    hop_z = ((me >> 1) - (owner >> 1)) & 3
    hop_y = ((me >> 3) - (owner >> 3)) & 3
    place_z = jnp.where(hop_z > 1, 5 - hop_z, hop_z)
    place_y = jnp.where(hop_y > 1, 5 - hop_y, hop_y)
    slot = (((me ^ owner) & 1) * 4 + place_y) * 4 + place_z
    far_at[...] = slot * OWN + (far & 7)

    lane = lanes(2 * PROBES)
    acc = jnp.zeros((PROBES, 128), F32)
    fields = []
    for i in range(OWN):
        raw = jnp.concatenate([probes[i, 0], probes[i, 1]], axis=0)
        field = jnp.where(lane < rows[i], raw, 0.0)
        base[i] = field
        fields.append(field)
        square = field * field
        acc = acc + square[:PROBES] + square[PROBES:]
    wide = []
    for i in range(OWN):
        high, low = high_low(paired(fields[i]))
        basis = col_basis[i]
        wide.append(coefficients(high, basis) + coefficients(low, basis))
    pay[0:32] = side_by_side(wide[:4]).astype(BF16)
    pay[32:64] = side_by_side(wide[4:]).astype(BF16)
    pay[STAT:PAY] = three_way(lane_sum(acc), 0).astype(BF16)


def pack_kernel(first, coupling, packed):
    for i in range(packed.shape[0]):
        for g in range(FMAX // 4):
            four = [coupling[first + i, 4 * g + f].reshape(2 * RANK, RANK) for f in range(4)]
            high, low = high_low(jnp.concatenate(four, axis=1))
            packed[i, :, 128 * g : 128 * g + 128] = jnp.concatenate([high, low], axis=0)


def near_kernel(first, split, fill, near_at, near_count, *refs):
    if fill:
        own, partner, other, blocks, near, table = refs
        for group, ref in enumerate((own, partner, other)):
            for i in range(OWN):
                field = ref[i].astype(F32)
                if split:
                    high, low = high_low(paired(field))
                    table[OWN * group + i] = jnp.concatenate([high, low], axis=0)
                else:
                    table[OWN * group + i] = paired(field).astype(BF16)
    else:
        table, blocks, near = refs
    count = near.shape[0]
    acc = [jnp.zeros((128, table.shape[1]), F32) for _ in range(count)]
    for k in range(KMAX):
        for i in range(count):
            vec = table[near_at[first + i, k]]
            vec = jnp.where(k < near_count[first + i], vec, jnp.zeros_like(vec))
            mat = jnp.concatenate([blocks[first + i, k, 0], blocks[first + i, k, 1]], axis=1)
            acc[i] = acc[i] + dot_nt(mat, vec)
    for i in range(count):
        out = jnp.transpose(acc[i])
        near[i] = out[:32] + out[32:] if split else out


def far_fields(far_at, mine, other, packs, row_basis, table, masks):
    for half, ref in enumerate((mine, other)):
        for slot in range(16):
            at = 2 * (16 * half + slot)
            table[at : at + 2] = ref[slot, 0:STAT].reshape(2, RANK, 128)
    block = lanes(RANK) // RANK
    for b in range(4):
        masks[b] = jnp.where(block == b, 1.0, 0.0).astype(BF16)
    folded = []
    for i in range(OWN):
        rows = []
        for f in range(FMAX):
            at = far_at[i, f]
            rows.append(table[at >> 2] * masks[at & 3])
        packed = packs[i // (OWN // 2)]
        acc = dot_nn(packed[i % (OWN // 2)], jnp.concatenate(rows, axis=0))
        folded.append(acc[:64] + acc[64:])
    both = jnp.concatenate(folded, axis=0)
    both = both + pltpu.roll(both, 64, 1)
    both = both + pltpu.roll(both, 32, 1)
    both = both.reshape(OWN, 2, RANK, 128)
    real, imag = (both[:, c].reshape(OWN * RANK, 128) for c in range(2))
    lane = lanes(OWN * RANK)
    sign = jnp.where((lane // PROBES) % 2 == 0, -1.0, 1.0)
    farcoef = real + sign * pltpu.roll(imag, PROBES, 1)
    turned = sign * pltpu.roll(farcoef, PROBES, 1)
    chosen = []
    for value in (farcoef, turned):
        high = value.astype(BF16).astype(F32)
        chosen.append(jnp.where(lane < 32, high, value - high).astype(BF16))
    out = []
    for i in range(OWN):
        span = slice(RANK * i, RANK * i + RANK)
        left = jnp.concatenate([chosen[0][span], chosen[1][span]], axis=0)
        out.append(dot_tn(left, row_basis[i].reshape(2 * RANK, 128)))
    return [x[0:32] + x[32:64] for x in out]


def image_kernel(far_at, rows, mine, other, *refs):
    pack_a, pack_b, row_basis, col_basis, *nears, base, image, narrow, pay, keep, table, masks = refs
    far = far_fields(far_at, mine, other, (pack_a, pack_b), row_basis, table, masks)
    beta = jnp.sqrt(column_of(gathered_stat(mine, other), 0, 32, 64) + 1e-06)
    inverse = twice(1.0 / beta)
    lane = lanes(2 * PROBES)
    near = [ref[i] for ref in nears for i in range(ref.shape[0])]
    acc_re = jnp.zeros((PROBES, 128), F32)
    acc_im = jnp.zeros((PROBES, 128), F32)
    values = []
    for i in range(OWN):
        value = jnp.where(lane < rows[i], near[i] + far[i], 0.0) * inverse
        values.append(value)
        image[i] = value
        narrow[i] = value.astype(BF16)
    wide = [coefficients(paired(values[i]).astype(BF16), col_basis[i]) for i in range(OWN)]
    for i in range(OWN):
        first = base[i] * inverse
        vr, vi = first[:PROBES], first[PROBES:]
        wr, wi = values[i][:PROBES], values[i][PROBES:]
        acc_re = acc_re + vr * wr + vi * wi
        acc_im = acc_im + vr * wi - vi * wr
    pay[0:32] = side_by_side(wide[:4]).astype(BF16)
    pay[32:64] = side_by_side(wide[4:]).astype(BF16)
    pay[STAT:PAY] = (three_way(lane_sum(acc_re), 0) + three_way(lane_sum(acc_im), 1)).astype(BF16)
    keep[...] = jnp.broadcast_to(beta, (PROBES, 128))


def inner_kernel(far_at, rows, mine, other, *refs):
    pack_a, pack_b, row_basis, *nears, base, image, keep, sums, head, table, masks = refs
    far = far_fields(far_at, mine, other, (pack_a, pack_b), row_basis, table, masks)
    stat = gathered_stat(mine, other)
    hr = column_of(stat, 0, 32, 64)
    hi = column_of(stat, 1, 33, 65)
    beta = column_of(keep[...], 0)
    inverse = twice(1.0 / beta)
    lane = lanes(2 * PROBES)
    near = [ref[i] for ref in nears for i in range(ref.shape[0])]

    def times_h(field):
        re, im = field[:PROBES], field[PROBES:]
        return jnp.concatenate([hr * re - hi * im, hr * im + hi * re], axis=0)

    acc = [jnp.zeros((PROBES, 128), F32) for _ in range(9)]
    left, right = [], []
    for i in range(OWN):
        second = jnp.where(lane < rows[i], near[i] + far[i], 0.0)
        w = image[i]
        b = base[i]
        v = b * inverse
        t = w - times_h(v)
        u = second - times_h(w)
        wr, wi, ur, ui = w[:PROBES], w[PROBES:], u[:PROBES], u[PROBES:]
        br, bi, tr, ti = b[:PROBES], b[PROBES:], t[:PROBES], t[PROBES:]
        vr, vi = v[:PROBES], v[PROBES:]
        terms = (
            tr * tr + ti * ti,
            wr * ur + wi * ui,
            wr * ui - wi * ur,
            ur * ur + ui * ui,
            ur * br + ui * bi,
            ur * bi - ui * br,
            wr * wr + wi * wi,
            wr * br + wi * bi,
            wr * bi - wi * br,
        )
        acc = [a + x for a, x in zip(acc, terms)]
        left.append(
            jnp.concatenate(
                [jnp.concatenate([vr, vi], axis=1), jnp.concatenate([tr, ti], axis=1)], axis=0
            )
        )
        right.append(
            jnp.concatenate(
                [jnp.concatenate([br, bi], axis=1), jnp.concatenate([-bi, br], axis=1)], axis=0
            )
        )
    mom = lax.dot_general(
        jnp.concatenate(left, axis=1),
        jnp.concatenate(right, axis=1),
        (((1,), (1,)), ((), ())),
        precision=lax.Precision.HIGHEST,
        preferred_element_type=F32,
    )
    short = lanes(PROBES)
    wide = jnp.concatenate([mom, jnp.zeros((2 * PROBES, 96), F32)], axis=1)
    tile = jnp.where(
        (short >= 16) & (short < 48), pltpu.roll(wide[:PROBES], 16, 1), 0.0
    ) + jnp.where((short >= 48) & (short < 80), pltpu.roll(wide[PROBES:], 48, 1), 0.0)
    for k, term in enumerate(acc):
        tile = tile + jnp.where(short == k, lane_sum(term), 0.0)
    sums[...] = tile
    head[...] = jnp.where(short == 0, beta, jnp.where(short == 1, hr, jnp.where(short == 2, hi, 0.0)))


def final_kernel(weight, sums, head, base, image, solution, moment, arnoldi):
    tile = sums[0]
    for slot in range(1, sums.shape[0]):
        tile = tile + sums[slot]
    top = head[...]
    beta, hr, hi = (column_of(top, k) for k in range(3))
    t2, g12r, g12i, g22, q2r, q2i, g11, q1r, q1i = (column_of(tile, k) for k in range(9))
    size = jnp.sqrt(t2 + 1e-06)
    inv = 1.0 / size
    g12r, g12i, q2r, q2i = g12r * inv, g12i * inv, q2r * inv, q2i * inv
    g22 = g22 * inv * inv
    det = g11 * g22 - (g12r * g12r + g12i * g12i)
    y1r = (g22 * q1r - (g12r * q2r - g12i * q2i)) / det
    y1i = (g22 * q1i - (g12r * q2i + g12i * q2r)) / det
    y2r = (g11 * q2r - (g12r * q1r + g12i * q1i)) / det * inv
    y2i = (g11 * q2i - (g12r * q1i - g12i * q1r)) / det * inv
    wr, wi = weight[0], weight[1]
    factor = 1.0 / (256 * 128)
    inverse = 1.0 / beta
    for i in range(OWN):
        vr, vi = base[i, :PROBES] * inverse, base[i, PROBES:] * inverse
        tr = image[i, :PROBES] - (hr * vr - hi * vi)
        ti = image[i, PROBES:] - (hr * vi + hi * vr)
        xr = (y1r * vr - y1i * vi) + (y2r * tr - y2i * ti)
        xi = (y1r * vi + y1i * vr) + (y2r * ti + y2i * tr)
        solution[i, 0] = wr * xr - wi * xi
        solution[i, 1] = wr * xi + wi * xr
    lane = lanes(PROBES)
    sign = jnp.where(lane < 32, -1.0, 1.0)

    def turned(x):
        return sign * jnp.where(lane < 32, pltpu.roll(x, 112, 1), pltpu.roll(x, 16, 1))

    late = pltpu.roll(tile, 96, 1)
    mom = (y1r * tile + y1i * turned(tile)) + (y2r * late + y2i * turned(late))
    mom = (wr * mom + wi * turned(mom)) * factor
    root = jnp.sqrt(jnp.full((1, 1), factor, F32))
    out = jnp.where((lane >= 16) & (lane < 48), mom, 0.0)
    for k, column in enumerate((beta * root, hr, hi, size)):
        out = jnp.where(lane == k, column, out)
    turned_out = jnp.transpose(out)
    moment[0] = turned_out[16:32]
    moment[1] = turned_out[32:48]
    arnoldi[...] = turned_out[0:4]


def shape(dims, dtype=F32):
    return jax.ShapeDtypeStruct(dims, dtype)


def params(mib):
    return pltpu.CompilerParams(vmem_limit_bytes=mib << 20)


def z_step(d):
    return [(i, (i & ~6) | ((((i >> 1) + d) & 3) << 1)) for i in range(32)]


def y_step(d):
    return [(i, (i & 7) | ((((i >> 3) + d) & 3) << 3)) for i in range(32)]


CORE = [(i, i ^ 1) for i in range(32)]
SIDE = [(i, i + 1 if i % 2 else i - 1) for i in range(1, 31)]


def send(x, pairs):
    return lax.ppermute(x, "clus", pairs)


def gather_ring(x, step):
    low = send(x, step(1))
    high = send(x, step(3))
    last = send(low, step(1))
    return jnp.concatenate([x, low, high, last], axis=0)


def gather_all(pay):
    four = gather_ring(pay[None], z_step)
    mine = gather_ring(four, y_step)
    return mine, send(mine, CORE)


def shards(
    probes,
    near_blocks,
    near_list,
    near_count,
    cluster_rows,
    row_basis,
    col_basis,
    far_list,
    far_coupling,
    weight,
):
    base, pay, near_at, far_at = pl.pallas_call(
        front_kernel,
        out_shape=(
            shape((OWN, 32, 128)),
            shape((PAY, 128), BF16),
            shape((OWN, KMAX), jnp.int32),
            shape((OWN, FMAX), jnp.int32),
        ),
        in_specs=[SMEM] + [VMEM] * 4,
        out_specs=(VMEM,) * 4,
        compiler_params=params(4),
        name="front",
    )(cluster_rows, near_list, far_list, probes, col_basis)

    def pack(first):
        half = OWN // 2
        return pl.pallas_call(
            functools.partial(pack_kernel, first),
            out_shape=shape((half, 128, 1024), BF16),
            in_specs=[VMEM],
            out_specs=VMEM,
            compiler_params=params(10),
            cost_estimate=pl.CostEstimate(flops=1 << 20, bytes_accessed=5 << 20, transcendentals=0),
            name="pack",
        )(far_coupling)

    def near_products(split, field):
        partner = send(field, CORE)
        other = send(field, SIDE)
        height = 64 if split else 32
        nears, table, at = [], None, 0
        for part, size in enumerate(NEAR_SPLIT):
            fill = part == 0
            out = pl.pallas_call(
                functools.partial(near_kernel, at, split, fill),
                out_shape=(shape((size, 32, 128)),)
                + ((shape((3 * OWN, height, 256), BF16),) if fill else ()),
                in_specs=[SMEM, SMEM] + [VMEM] * (4 if fill else 2),
                out_specs=(VMEM,) * (2 if fill else 1),
                compiler_params=params(16),
                cost_estimate=pl.CostEstimate(
                    flops=size * KMAX * 8 * 128 * 128 * 16,
                    bytes_accessed=size * KMAX << 16,
                    transcendentals=0,
                ),
                name="near",
            )(near_at, near_count, *((field, partner, other) if fill else (table,)), near_blocks)
            if fill:
                table = out[1]
            nears.append(out[0])
            at += size
        return nears

    packs = (pack(0), pack(OWN // 2))
    nears = near_products(True, base)
    mine, other = gather_all(pay)
    scratch = [pltpu.VMEM((64, RANK, 128), BF16), pltpu.VMEM((4, RANK, 128), BF16)]
    image, narrow, pay_two, keep = pl.pallas_call(
        image_kernel,
        out_shape=(
            shape((OWN, 32, 128)),
            shape((OWN, 32, 128), BF16),
            shape((PAY, 128), BF16),
            shape((PROBES, 128)),
        ),
        in_specs=[SMEM, SMEM] + [VMEM] * (7 + len(nears)),
        out_specs=(VMEM,) * 4,
        scratch_shapes=scratch,
        compiler_params=params(10),
        name="image",
    )(far_at, cluster_rows, mine, other, *packs, row_basis, col_basis, *nears, base)

    nears = near_products(False, narrow)
    mine, other = gather_all(pay_two)
    sums, head = pl.pallas_call(
        inner_kernel,
        out_shape=(shape((PROBES, 128)), shape((PROBES, 128))),
        in_specs=[SMEM, SMEM] + [VMEM] * (8 + len(nears)),
        out_specs=(VMEM, VMEM),
        scratch_shapes=scratch,
        compiler_params=params(10),
        name="inner",
    )(far_at, cluster_rows, mine, other, *packs, row_basis, *nears, base, image, keep)

    spread = jnp.broadcast_to(sums[None], (32, PROBES, 128))
    return pl.pallas_call(
        final_kernel,
        out_shape=(shape((OWN, 2, PROBES, 128)), shape((2, PROBES, PROBES)), shape((4, PROBES))),
        in_specs=[SMEM] + [VMEM] * 4,
        out_specs=(VMEM,) * 3,
        compiler_params=params(4),
        name="final",
    )(weight, lax.all_to_all(spread, "clus", 0, 0), head, base, image)


def solution(mesh):
    in_specs = (
        P("clus", None, None, None),
        P(("contour", "clus"), None, None, None, None),
        P("clus", None),
        P("clus"),
        P("clus"),
        P(("contour", "clus"), None, None, None),
        P(("contour", "clus"), None, None, None),
        P("clus", None),
        P(("contour", "clus"), None, None, None, None),
        P("contour"),
    )
    out_specs = (
        P(("contour", "clus"), None, None, None),
        P("contour", None, None),
        P("contour", None),
    )
    return jax.shard_map(shards, mesh=mesh, in_specs=in_specs, out_specs=out_specs, check_vma=False)
```

profile of v0, /device:TPU:0, one launch (start us, length us, event | category | flops | bytes accessed | tf_op | source)
XLA Modules:
  0.0 96.5 jit_solution(9547999073794987477)
XLA Ops:
  0.7 1.0 %copy-done.3 = bf16[8,2,32,128]{3,2,1,0:T(8,128)(2,1)S(1)} copy-done((bf16[8,2,32,128]{3,2,1,0:T(8,128)(2,1)S(1)}, bf16[8,2,32,128]{3,2,1,0:T(8,128)(2,1)}, u32[]{:S(2)}) %copy-start.3) | copy-done | bytes 131096
  1.7 1.1 %copy-done.5 = f32[8,2,16,128]{3,2,1,0:T(8,128)S(1)} copy-done((f32[8,2,16,128]{3,2,1,0:T(8,128)S(1)}, f32[8,2,16,128]{3,2,1,0:T(8,128)}, u32[]{:S(2)}) %copy-start.5) | copy-done | bytes 131096
  2.8 1.0 %copy-done.7 = s32[8]{0:T(128)S(1)} copy-done((s32[8]{0:T(128)S(1)}, s32[8]{0:T(128)}, u32[]{:S(2)}) %copy-start.7) | copy-done | bytes 56
  5.5 1.0 %front.1 = (f32[8,32,128]{2,1,0:T(8,128)S(1)}, bf16[80,128]{1,0:T(8,128)(2,1)S(1)}, s32[8,27]{1,0:T(8,128)S(1)}, s32[8,32]{1,0:T(8,128)S(1)}) custom-call(s32[8]{0:T(128)S(1)} %copy-done.7, s32[8,27]{1,0:T(8,128)S(1)} %copy-done.9, s32[8,32]{1,0:T(8,128)S(1)} %copy-done.10, f32[8,2,16,128]{3,2,1,0:T(8,128)S(1)} %copy-done.5, ...), custom_call_target="tpu_custom_call" | custom-call | tf_op jit(solution)/shard_map/front/pallas_call | solution.py:402
  6.5 2.1 %collective-permute-start = (bf16[1,80,128]{2,1,0:T(8,128)(2,1)S(1)}, bf16[1,80,128]{2,1,0:T(8,128)(2,1)S(1)}, u32[]{:S(2)}, u32[]{:S(2)}) collective-permute-start(bf16[1,80,128]{2,1,0:T(8,128)(2,1)S(1)} %bitcast.7), channel_id=1, source_target_pairs={{0,2},{1,3},{2,4},{3,5},{4,6},{5,7},{6,0},{7,1},{8,10},{9,11},{10,... | collective-permute-start | bytes 61448 | tf_op jit(solution)/shard_map/ppermute | solution.py:374
  8.6 2.2 %collective-permute-start.1 = (bf16[1,80,128]{2,1,0:T(8,128)(2,1)S(1)}, bf16[1,80,128]{2,1,0:T(8,128)(2,1)S(1)}, u32[]{:S(2)}, u32[]{:S(2)}) collective-permute-start(bf16[1,80,128]{2,1,0:T(8,128)(2,1)S(1)} %bitcast.8), channel_id=1, source_target_pairs={{0,6},{1,7},{2,0},{3,1},{4,2},{5,3},{6,4},{7,5},{8,14},{9,15},{10,... | collective-permute-start | bytes 61448 | tf_op jit(solution)/shard_map/ppermute | solution.py:374
  10.8 1.7 %collective-permute-done = bf16[1,80,128]{2,1,0:T(8,128)(2,1)S(1)} collective-permute-done((bf16[1,80,128]{2,1,0:T(8,128)(2,1)S(1)}, bf16[1,80,128]{2,1,0:T(8,128)(2,1)S(1)}, u32[]{:S(2)}, u32[]{:S(2)}) %collective-permute-start) | collective-permute-done | bytes 20512 | tf_op jit(solution)/shard_map/ppermute | solution.py:374
  12.5 5.0 %collective-permute-done.2 = bf16[1,80,128]{2,1,0:T(8,128)(2,1)S(1)} collective-permute-done((bf16[1,80,128]{2,1,0:T(8,128)(2,1)S(1)}, bf16[1,80,128]{2,1,0:T(8,128)(2,1)S(1)}, u32[]{:S(2)}, u32[]{:S(2)}) %collective-permute-start.2) | collective-permute-done | bytes 20512 | tf_op jit(solution)/shard_map/ppermute | solution.py:374
  17.5 1.6 %collective-permute-start.3 = (bf16[4,80,128]{2,1,0:T(8,128)(2,1)S(1)}, bf16[4,80,128]{2,1,0:T(8,128)(2,1)S(1)}, u32[]{:S(2)}, u32[]{:S(2)}) collective-permute-start(bf16[4,80,128]{2,1,0:T(8,128)(2,1)S(1)} %pad_maximum_fusion), channel_id=1, source_target_pairs={{0,8},{1,9},{2,10},{3,11},{4,12},{5,13},{6,14},{7,15},{8,16},{9,17... | collective-permute-start | bytes 245768 | tf_op jit(solution)/shard_map/ppermute | solution.py:374
  19.2 1.7 %collective-permute-start.4 = (bf16[4,80,128]{2,1,0:T(8,128)(2,1)S(1)}, bf16[4,80,128]{2,1,0:T(8,128)(2,1)S(1)}, u32[]{:S(2)}, u32[]{:S(2)}) collective-permute-start(bf16[4,80,128]{2,1,0:T(8,128)(2,1)S(1)} %pad_maximum_fusion), channel_id=1, source_target_pairs={{0,24},{1,25},{2,26},{3,27},{4,28},{5,29},{6,30},{7,31},{8,0},{9,1... | collective-permute-start | bytes 245768 | tf_op jit(solution)/shard_map/ppermute | solution.py:374
  20.8 2.4 %collective-permute-done.3 = bf16[4,80,128]{2,1,0:T(8,128)(2,1)S(1)} collective-permute-done((bf16[4,80,128]{2,1,0:T(8,128)(2,1)S(1)}, bf16[4,80,128]{2,1,0:T(8,128)(2,1)S(1)}, u32[]{:S(2)}, u32[]{:S(2)}) %collective-permute-start.3) | collective-permute-done | bytes 81952 | tf_op jit(solution)/shard_map/ppermute | solution.py:374
  23.2 1.1 %collective-permute-start.5 = (bf16[4,80,128]{2,1,0:T(8,128)(2,1)S(1)}, bf16[4,80,128]{2,1,0:T(8,128)(2,1)S(1)}, u32[]{:S(2)}, u32[]{:S(2)}) collective-permute-start(bf16[4,80,128]{2,1,0:T(8,128)(2,1)S(1)} %collective-permute-done.3), channel_id=1, source_target_pairs={{0,8},{1,9},{2,10},{3,11},{4,12},{5,13},{6,14},{7,15},{8,16},{9,17... | collective-permute-start | bytes 245768 | tf_op jit(solution)/shard_map/ppermute | solution.py:374
  24.4 4.5 %collective-permute-done.5 = bf16[4,80,128]{2,1,0:T(8,128)(2,1)S(1)} collective-permute-done((bf16[4,80,128]{2,1,0:T(8,128)(2,1)S(1)}, bf16[4,80,128]{2,1,0:T(8,128)(2,1)S(1)}, u32[]{:S(2)}, u32[]{:S(2)}) %collective-permute-start.5) | collective-permute-done | bytes 81952 | tf_op jit(solution)/shard_map/ppermute | solution.py:374
  30.2 3.4 %copy-done.1 = f32[8,32,2,32,32]{4,3,2,1,0:T(8,128)S(1)} copy-done((f32[8,32,2,32,32]{4,3,2,1,0:T(8,128)S(1)}, f32[8,32,2,32,32]{4,3,2,1,0:T(8,128)}, u32[]{:S(2)}) %copy-start.1) | copy-done | bytes 2097176
  35.4 2.2 %near.6 = (f32[3,32,128]{2,1,0:T(8,128)S(1)}, bf16[24,64,256]{2,1,0:T(8,128)(2,1)S(1)}) custom-call(s32[8,27]{1,0:T(8,128)S(1)} %get-tuple-element.19.near_at, s32[8]{0:T(128)S(1)} %copy-done.6, f32[8,32,128]{2,1,0:T(8,128)S(1)} %get-tuple-element.20.refs_0_.refs_7_.refs_6_.base, f32[8,32,128]{2,1,0:T(8,128)S(1)} %collective-permute-done.7.refs_1_, ...), custom_call_target="tpu_custom_call" | custom-call | flops 169869312 | bytes 5308416 | tf_op jit(solution)/shard_map/near/pallas_call | solution.py:435
  37.6 1.7 %near.8.refs_6_ = f32[2,32,128]{2,1,0:T(8,128)S(1)} custom-call(s32[8,27]{1,0:T(8,128)S(1)} %get-tuple-element.19.near_at, s32[8]{0:T(128)S(1)} %copy-done.6, bf16[24,64,256]{2,1,0:T(8,128)(2,1)S(1)} %get-tuple-element.22.refs_0_, bf16[8,27,2,128,128]{4,3,2,1,0:T(8,128)(2,1)S(1)} %copy-done), custom_call_target="tpu_custom_call" | custom-call | flops 113246208 | bytes 3538944 | tf_op jit(solution)/shard_map/near/pallas_call | solution.py:435
  39.4 2.2 %near.7.refs_5_ = f32[3,32,128]{2,1,0:T(8,128)S(1)} custom-call(s32[8,27]{1,0:T(8,128)S(1)} %get-tuple-element.19.near_at, s32[8]{0:T(128)S(1)} %copy-done.6, bf16[24,64,256]{2,1,0:T(8,128)(2,1)S(1)} %get-tuple-element.22.refs_0_, bf16[8,27,2,128,128]{4,3,2,1,0:T(8,128)(2,1)S(1)} %copy-done), custom_call_target="tpu_custom_call" | custom-call | flops 169869312 | bytes 5308416 | tf_op jit(solution)/shard_map/near/pallas_call | solution.py:435
  41.6 2.3 %image.1 = (f32[8,32,128]{2,1,0:T(8,128)S(1)}, bf16[8,32,128]{2,1,0:T(8,128)(2,1)S(1)}, bf16[80,128]{1,0:T(8,128)(2,1)S(1)}, f32[16,128]{1,0:T(8,128)S(1)}) custom-call(s32[8,32]{1,0:T(8,128)S(1)} %get-tuple-element.17.far_at, s32[8]{0:T(128)S(1)} %copy-done.8, bf16[16,80,128]{2,1,0:T(8,128)(2,1)S(1)} %constant_dynamic-update-slice_fusion.mine, ...), custom_call_target="tpu_custom_call" | custom-call | tf_op jit(solution)/shard_map/image/pallas_call | solution.py:459
  43.8 3.0 %collective-permute-start.9 = (bf16[1,80,128]{2,1,0:T(8,128)(2,1)S(1)}, bf16[1,80,128]{2,1,0:T(8,128)(2,1)S(1)}, u32[]{:S(2)}, u32[]{:S(2)}) collective-permute-start(bf16[1,80,128]{2,1,0:T(8,128)(2,1)S(1)} %bitcast.4), channel_id=1, source_target_pairs={{0,2},{1,3},{2,4},{3,5},{4,6},{5,7},{6,0},{7,1},{8,10},{9,11},{10,... | collective-permute-start | bytes 61448 | tf_op jit(solution)/shard_map/ppermute | solution.py:374
  47.1 1.8 %collective-permute-done.9 = bf16[1,80,128]{2,1,0:T(8,128)(2,1)S(1)} collective-permute-done((bf16[1,80,128]{2,1,0:T(8,128)(2,1)S(1)}, bf16[1,80,128]{2,1,0:T(8,128)(2,1)S(1)}, u32[]{:S(2)}, u32[]{:S(2)}) %collective-permute-start.9) | collective-permute-done | bytes 20512 | tf_op jit(solution)/shard_map/ppermute | solution.py:374
  48.9 1.7 %collective-permute-start.11 = (bf16[1,80,128]{2,1,0:T(8,128)(2,1)S(1)}, bf16[1,80,128]{2,1,0:T(8,128)(2,1)S(1)}, u32[]{:S(2)}, u32[]{:S(2)}) collective-permute-start(bf16[1,80,128]{2,1,0:T(8,128)(2,1)S(1)} %collective-permute-done.9), channel_id=1, source_target_pairs={{0,2},{1,3},{2,4},{3,5},{4,6},{5,7},{6,0},{7,1},{8,10},{9,11},{10,... | collective-permute-start | bytes 61448 | tf_op jit(solution)/shard_map/ppermute | solution.py:374
  50.7 3.2 %collective-permute-done.11 = bf16[1,80,128]{2,1,0:T(8,128)(2,1)S(1)} collective-permute-done((bf16[1,80,128]{2,1,0:T(8,128)(2,1)S(1)}, bf16[1,80,128]{2,1,0:T(8,128)(2,1)S(1)}, u32[]{:S(2)}, u32[]{:S(2)}) %collective-permute-start.11) | collective-permute-done | bytes 20512 | tf_op jit(solution)/shard_map/ppermute | solution.py:374
  53.9 3.3 %collective-permute-start.12 = (bf16[4,80,128]{2,1,0:T(8,128)(2,1)S(1)}, bf16[4,80,128]{2,1,0:T(8,128)(2,1)S(1)}, u32[]{:S(2)}, u32[]{:S(2)}) collective-permute-start(bf16[4,80,128]{2,1,0:T(8,128)(2,1)S(1)} %pad_maximum_fusion.1), channel_id=1, source_target_pairs={{0,8},{1,9},{2,10},{3,11},{4,12},{5,13},{6,14},{7,15},{8,16},{9,17... | collective-permute-start | bytes 245768 | tf_op jit(solution)/shard_map/ppermute | solution.py:374
  57.9 2.3 %collective-permute-done.12 = bf16[4,80,128]{2,1,0:T(8,128)(2,1)S(1)} collective-permute-done((bf16[4,80,128]{2,1,0:T(8,128)(2,1)S(1)}, bf16[4,80,128]{2,1,0:T(8,128)(2,1)S(1)}, u32[]{:S(2)}, u32[]{:S(2)}) %collective-permute-start.12) | collective-permute-done | bytes 81952 | tf_op jit(solution)/shard_map/ppermute | solution.py:374
  60.2 1.9 %collective-permute-start.14 = (bf16[4,80,128]{2,1,0:T(8,128)(2,1)S(1)}, bf16[4,80,128]{2,1,0:T(8,128)(2,1)S(1)}, u32[]{:S(2)}, u32[]{:S(2)}) collective-permute-start(bf16[4,80,128]{2,1,0:T(8,128)(2,1)S(1)} %collective-permute-done.12), channel_id=1, source_target_pairs={{0,8},{1,9},{2,10},{3,11},{4,12},{5,13},{6,14},{7,15},{8,16},{9,17... | collective-permute-start | bytes 245768 | tf_op jit(solution)/shard_map/ppermute | solution.py:374
  62.2 3.7 %collective-permute-done.14 = bf16[4,80,128]{2,1,0:T(8,128)(2,1)S(1)} collective-permute-done((bf16[4,80,128]{2,1,0:T(8,128)(2,1)S(1)}, bf16[4,80,128]{2,1,0:T(8,128)(2,1)S(1)}, u32[]{:S(2)}, u32[]{:S(2)}) %collective-permute-start.14) | collective-permute-done | bytes 81952 | tf_op jit(solution)/shard_map/ppermute | solution.py:374
  67.7 2.2 %near.9 = (f32[3,32,128]{2,1,0:T(8,128)S(1)}, bf16[24,32,256]{2,1,0:T(8,128)(2,1)S(1)}) custom-call(s32[8,27]{1,0:T(8,128)S(1)} %get-tuple-element.19.near_at, s32[8]{0:T(128)S(1)} %copy-done.6, bf16[8,32,128]{2,1,0:T(8,128)(2,1)S(1)} %get-tuple-element.24.refs_0_, bf16[8,32,128]{2,1,0:T(8,128)(2,1)S(1)} %collective-permute-done.16.refs_1_, ...), custom_call_target="tpu_custom_call" | custom-call | flops 169869312 | bytes 5308416 | tf_op jit(solution)/shard_map/near/pallas_call | solution.py:435
  69.9 1.7 %near.11.refs_5_ = f32[2,32,128]{2,1,0:T(8,128)S(1)} custom-call(s32[8,27]{1,0:T(8,128)S(1)} %get-tuple-element.19.near_at, s32[8]{0:T(128)S(1)} %copy-done.6, bf16[24,32,256]{2,1,0:T(8,128)(2,1)S(1)} %get-tuple-element.26.refs_0_, bf16[8,27,2,128,128]{4,3,2,1,0:T(8,128)(2,1)S(1)} %copy-done), custom_call_target="tpu_custom_call" | custom-call | flops 113246208 | bytes 3538944 | tf_op jit(solution)/shard_map/near/pallas_call | solution.py:435
  71.6 2.2 %near.10.refs_4_ = f32[3,32,128]{2,1,0:T(8,128)S(1)} custom-call(s32[8,27]{1,0:T(8,128)S(1)} %get-tuple-element.19.near_at, s32[8]{0:T(128)S(1)} %copy-done.6, bf16[24,32,256]{2,1,0:T(8,128)(2,1)S(1)} %get-tuple-element.26.refs_0_, bf16[8,27,2,128,128]{4,3,2,1,0:T(8,128)(2,1)S(1)} %copy-done), custom_call_target="tpu_custom_call" | custom-call | flops 169869312 | bytes 5308416 | tf_op jit(solution)/shard_map/near/pallas_call | solution.py:435
  73.8 2.6 %inner.1 = (f32[16,128]{1,0:T(8,128)S(1)}, f32[16,128]{1,0:T(8,128)S(1)}) custom-call(s32[8,32]{1,0:T(8,128)S(1)} %get-tuple-element.17.far_at, s32[8]{0:T(128)S(1)} %copy-done.8, bf16[16,80,128]{2,1,0:T(8,128)(2,1)S(1)} %constant_dynamic-update-slice_fusion.7.mine, bf16[16,80,128]{2,1,0:T(8,128)(2,1)S(1)} %collective-permute-done.15.other, ...), custom_call_target="tpu_custom_call" | custom-call | tf_op jit(solution)/shard_map/inner/pallas_call | solution.py:476
  76.4 18.6 %all_to_all.5.sums = f32[32,16,128]{2,1,0:T(8,128)S(1)} all-to-all(f32[32,16,128]{2,1,0:T(8,128)S(1)} %broadcast_in_dim.14), channel_id=1, replica_groups=mesh['contour'=4,'clus'=32] {'clus'}, dimensions={0} | all-to-all | bytes 524288 | tf_op jit(solution)/shard_map/all_to_all | solution.py:494
  95.0 1.5 %final.1 = (f32[8,2,16,128]{3,2,1,0:T(8,128)}, f32[2,16,16]{2,1,0:T(8,128)}, f32[4,16]{1,0:T(4,128)}) custom-call(f32[2]{0:T(128)S(1)} %copy-done.11, f32[32,16,128]{2,1,0:T(8,128)S(1)} %all_to_all.5.sums, f32[16,128]{1,0:T(8,128)S(1)} %get-tuple-element.30.head, f32[8,32,128]{2,1,0:T(8,128)S(1)} %get-tuple-element.20.refs_0_.refs_7_.refs_6_.base, ...), custom_call_target="tpu_custom_call" | custom-call | tf_op jit(solution)/shard_map/final/pallas_call | solution.py:487
  (58 shorter events, 7.8 us)
Async XLA Ops:
  0.6 34.7 %copy-start = (bf16[8,27,2,128,128]{4,3,2,1,0:T(8,128)(2,1)S(1)}, bf16[8,27,2,128,128]{4,3,2,1,0:T(8,128)(2,1)}, u32[]{:S(2)}) copy-start(bf16[8,27,2,128,128]{4,3,2,1,0:T(8,128)(2,1)} %refs_1_.7) | copy-start | bytes 42467332
  0.6 1.1 %copy-start.3 = (bf16[8,2,32,128]{3,2,1,0:T(8,128)(2,1)S(1)}, bf16[8,2,32,128]{3,2,1,0:T(8,128)(2,1)}, u32[]{:S(2)}) copy-start(bf16[8,2,32,128]{3,2,1,0:T(8,128)(2,1)} %refs_3_.4) | copy-start | bytes 393220
  1.7 1.1 %copy-start.5 = (f32[8,2,16,128]{3,2,1,0:T(8,128)S(1)}, f32[8,2,16,128]{3,2,1,0:T(8,128)}, u32[]{:S(2)}) copy-start(f32[8,2,16,128]{3,2,1,0:T(8,128)} %probes.1) | copy-start | bytes 393220
  2.8 1.0 %copy-start.7 = (s32[8]{0:T(128)S(1)}, s32[8]{0:T(128)}, u32[]{:S(2)}) copy-start(s32[8]{0:T(128)} %rows.5) | copy-start | bytes 100
  3.8 0.9 copy-start.9
  4.7 0.8 copy-start.10
  6.5 6.0 %collective-permute-start = (bf16[1,80,128]{2,1,0:T(8,128)(2,1)S(1)}, bf16[1,80,128]{2,1,0:T(8,128)(2,1)S(1)}, u32[]{:S(2)}, u32[]{:S(2)}) collective-permute-start(bf16[1,80,128]{2,1,0:T(8,128)(2,1)S(1)} %bitcast.7), channel_id=1, source_target_pairs={{0,2},{1,3},{2,4},{3,5},{4,6},{5,7},{6,0},{7,1},{8,10},{9,11},{10,... | collective-permute-start | bytes 61448 | tf_op jit(solution)/shard_map/ppermute | solution.py:374
  8.6 3.9 %collective-permute-start.1 = (bf16[1,80,128]{2,1,0:T(8,128)(2,1)S(1)}, bf16[1,80,128]{2,1,0:T(8,128)(2,1)S(1)}, u32[]{:S(2)}, u32[]{:S(2)}) collective-permute-start(bf16[1,80,128]{2,1,0:T(8,128)(2,1)S(1)} %bitcast.8), channel_id=1, source_target_pairs={{0,6},{1,7},{2,0},{3,1},{4,2},{5,3},{6,4},{7,5},{8,14},{9,15},{10,... | collective-permute-start | bytes 61448 | tf_op jit(solution)/shard_map/ppermute | solution.py:374
  12.5 5.0 %collective-permute-start.2 = (bf16[1,80,128]{2,1,0:T(8,128)(2,1)S(1)}, bf16[1,80,128]{2,1,0:T(8,128)(2,1)S(1)}, u32[]{:S(2)}, u32[]{:S(2)}) collective-permute-start(bf16[1,80,128]{2,1,0:T(8,128)(2,1)S(1)} %collective-permute-done), channel_id=1, source_target_pairs={{0,2},{1,3},{2,4},{3,5},{4,6},{5,7},{6,0},{7,1},{8,10},{9,11},{10,... | collective-permute-start | bytes 61448 | tf_op jit(solution)/shard_map/ppermute | solution.py:374
  17.5 5.7 %collective-permute-start.3 = (bf16[4,80,128]{2,1,0:T(8,128)(2,1)S(1)}, bf16[4,80,128]{2,1,0:T(8,128)(2,1)S(1)}, u32[]{:S(2)}, u32[]{:S(2)}) collective-permute-start(bf16[4,80,128]{2,1,0:T(8,128)(2,1)S(1)} %pad_maximum_fusion), channel_id=1, source_target_pairs={{0,8},{1,9},{2,10},{3,11},{4,12},{5,13},{6,14},{7,15},{8,16},{9,17... | collective-permute-start | bytes 245768 | tf_op jit(solution)/shard_map/ppermute | solution.py:374
  19.2 5.2 %collective-permute-start.4 = (bf16[4,80,128]{2,1,0:T(8,128)(2,1)S(1)}, bf16[4,80,128]{2,1,0:T(8,128)(2,1)S(1)}, u32[]{:S(2)}, u32[]{:S(2)}) collective-permute-start(bf16[4,80,128]{2,1,0:T(8,128)(2,1)S(1)} %pad_maximum_fusion), channel_id=1, source_target_pairs={{0,24},{1,25},{2,26},{3,27},{4,28},{5,29},{6,30},{7,31},{8,0},{9,1... | collective-permute-start | bytes 245768 | tf_op jit(solution)/shard_map/ppermute | solution.py:374
  23.2 5.7 %collective-permute-start.5 = (bf16[4,80,128]{2,1,0:T(8,128)(2,1)S(1)}, bf16[4,80,128]{2,1,0:T(8,128)(2,1)S(1)}, u32[]{:S(2)}, u32[]{:S(2)}) collective-permute-start(bf16[4,80,128]{2,1,0:T(8,128)(2,1)S(1)} %collective-permute-done.3), channel_id=1, source_target_pairs={{0,8},{1,9},{2,10},{3,11},{4,12},{5,13},{6,14},{7,15},{8,16},{9,17... | collective-permute-start | bytes 245768 | tf_op jit(solution)/shard_map/ppermute | solution.py:374
  28.9 12.7 %collective-permute-start.6 = (bf16[16,80,128]{2,1,0:T(8,128)(2,1)S(1)}, bf16[16,80,128]{2,1,0:T(8,128)(2,1)S(1)}, u32[]{:S(2)}, u32[]{:S(2)}) collective-permute-start(bf16[16,80,128]{2,1,0:T(8,128)(2,1)S(1)} %constant_dynamic-update-slice_fusion.mine), channel_id=1, source_target_pairs={{0,1},{1,0},{2,3},{3,2},{4,5},{5,4},{6,7},{7,6},{8,9},{9,8},{10,11... | collective-permute-start | bytes 983048 | tf_op jit(solution)/shard_map/ppermute | solution.py:374
  29.0 6.3 %collective-permute-start.7 = (f32[8,32,128]{2,1,0:T(8,128)S(1)}, f32[8,32,128]{2,1,0:T(8,128)S(1)}, u32[]{:S(2)}, u32[]{:S(2)}) collective-permute-start(f32[8,32,128]{2,1,0:T(8,128)S(1)} %get-tuple-element.20.refs_0_.refs_7_.refs_6_.base), channel_id=1, source_target_pairs={{0,1},{1,0},{2,3},{3,2},{4,5},{5,4},{6,7},{7,6},{8,9},{9,8},{10,11... | collective-permute-start | bytes 393224 | tf_op jit(solution)/shard_map/ppermute | solution.py:374
  29.5 5.8 %collective-permute-start.8 = (f32[8,32,128]{2,1,0:T(8,128)S(1)}, f32[8,32,128]{2,1,0:T(8,128)S(1)}, u32[]{:S(2)}, u32[]{:S(2)}) collective-permute-start(f32[8,32,128]{2,1,0:T(8,128)S(1)} %get-tuple-element.20.refs_0_.refs_7_.refs_6_.base), channel_id=1, source_target_pairs={{1,2},{2,1},{3,4},{4,3},{5,6},{6,5},{7,8},{8,7},{9,10},{10,9},{11,... | collective-permute-start | bytes 393224 | tf_op jit(solution)/shard_map/ppermute | solution.py:374
  30.2 3.4 %copy-start.1 = (f32[8,32,2,32,32]{4,3,2,1,0:T(8,128)S(1)}, f32[8,32,2,32,32]{4,3,2,1,0:T(8,128)}, u32[]{:S(2)}) copy-start(f32[8,32,2,32,32]{4,3,2,1,0:T(8,128)} %coupling.3) | copy-start | bytes 6291460
  33.5 1.8 %copy-start.6 = (s32[8]{0:T(128)S(1)}, s32[8]{0:T(128)}, u32[]{:S(2)}) copy-start(s32[8]{0:T(128)} %near_count.11) | copy-start | bytes 100
  37.6 3.9 %copy-start.2 = (bf16[8,2,32,128]{3,2,1,0:T(8,128)(2,1)S(1)}, bf16[8,2,32,128]{3,2,1,0:T(8,128)(2,1)}, u32[]{:S(2)}) copy-start(bf16[8,2,32,128]{3,2,1,0:T(8,128)(2,1)} %refs_2_.3) | copy-start | bytes 393220
  37.6 3.9 %copy-start.4 = (bf16[8,2,32,128]{3,2,1,0:T(8,128)(2,1)S(1)}, bf16[8,2,32,128]{3,2,1,0:T(8,128)(2,1)}, u32[]{:S(2)}) copy-start(bf16[8,2,32,128]{3,2,1,0:T(8,128)(2,1)} %refs_3_.4) | copy-start | bytes 393220
  37.6 3.9 %copy-start.8 = (s32[8]{0:T(128)S(1)}, s32[8]{0:T(128)}, u32[]{:S(2)}) copy-start(s32[8]{0:T(128)} %rows.5) | copy-start | bytes 100
  43.8 5.0 %collective-permute-start.9 = (bf16[1,80,128]{2,1,0:T(8,128)(2,1)S(1)}, bf16[1,80,128]{2,1,0:T(8,128)(2,1)S(1)}, u32[]{:S(2)}, u32[]{:S(2)}) collective-permute-start(bf16[1,80,128]{2,1,0:T(8,128)(2,1)S(1)} %bitcast.4), channel_id=1, source_target_pairs={{0,2},{1,3},{2,4},{3,5},{4,6},{5,7},{6,0},{7,1},{8,10},{9,11},{10,... | collective-permute-start | bytes 61448 | tf_op jit(solution)/shard_map/ppermute | solution.py:374
  46.9 3.8 %collective-permute-start.10 = (bf16[1,80,128]{2,1,0:T(8,128)(2,1)S(1)}, bf16[1,80,128]{2,1,0:T(8,128)(2,1)S(1)}, u32[]{:S(2)}, u32[]{:S(2)}) collective-permute-start(bf16[1,80,128]{2,1,0:T(8,128)(2,1)S(1)} %bitcast.5), channel_id=1, source_target_pairs={{0,6},{1,7},{2,0},{3,1},{4,2},{5,3},{6,4},{7,5},{8,14},{9,15},{10,... | collective-permute-start | bytes 61448 | tf_op jit(solution)/shard_map/ppermute | solution.py:374
  48.9 5.0 %collective-permute-start.11 = (bf16[1,80,128]{2,1,0:T(8,128)(2,1)S(1)}, bf16[1,80,128]{2,1,0:T(8,128)(2,1)S(1)}, u32[]{:S(2)}, u32[]{:S(2)}) collective-permute-start(bf16[1,80,128]{2,1,0:T(8,128)(2,1)S(1)} %collective-permute-done.9), channel_id=1, source_target_pairs={{0,2},{1,3},{2,4},{3,5},{4,6},{5,7},{6,0},{7,1},{8,10},{9,11},{10,... | collective-permute-start | bytes 61448 | tf_op jit(solution)/shard_map/ppermute | solution.py:374
  53.9 6.3 %collective-permute-start.12 = (bf16[4,80,128]{2,1,0:T(8,128)(2,1)S(1)}, bf16[4,80,128]{2,1,0:T(8,128)(2,1)S(1)}, u32[]{:S(2)}, u32[]{:S(2)}) collective-permute-start(bf16[4,80,128]{2,1,0:T(8,128)(2,1)S(1)} %pad_maximum_fusion.1), channel_id=1, source_target_pairs={{0,8},{1,9},{2,10},{3,11},{4,12},{5,13},{6,14},{7,15},{8,16},{9,17... | collective-permute-start | bytes 245768 | tf_op jit(solution)/shard_map/ppermute | solution.py:374
  57.2 5.0 %collective-permute-start.13 = (bf16[4,80,128]{2,1,0:T(8,128)(2,1)S(1)}, bf16[4,80,128]{2,1,0:T(8,128)(2,1)S(1)}, u32[]{:S(2)}, u32[]{:S(2)}) collective-permute-start(bf16[4,80,128]{2,1,0:T(8,128)(2,1)S(1)} %pad_maximum_fusion.1), channel_id=1, source_target_pairs={{0,24},{1,25},{2,26},{3,27},{4,28},{5,29},{6,30},{7,31},{8,0},{9,1... | collective-permute-start | bytes 245768 | tf_op jit(solution)/shard_map/ppermute | solution.py:374
  60.2 5.7 %collective-permute-start.14 = (bf16[4,80,128]{2,1,0:T(8,128)(2,1)S(1)}, bf16[4,80,128]{2,1,0:T(8,128)(2,1)S(1)}, u32[]{:S(2)}, u32[]{:S(2)}) collective-permute-start(bf16[4,80,128]{2,1,0:T(8,128)(2,1)S(1)} %collective-permute-done.12), channel_id=1, source_target_pairs={{0,8},{1,9},{2,10},{3,11},{4,12},{5,13},{6,14},{7,15},{8,16},{9,17... | collective-permute-start | bytes 245768 | tf_op jit(solution)/shard_map/ppermute | solution.py:374
  65.9 7.9 %collective-permute-start.15 = (bf16[16,80,128]{2,1,0:T(8,128)(2,1)S(1)}, bf16[16,80,128]{2,1,0:T(8,128)(2,1)S(1)}, u32[]{:S(2)}, u32[]{:S(2)}) collective-permute-start(bf16[16,80,128]{2,1,0:T(8,128)(2,1)S(1)} %constant_dynamic-update-slice_fusion.7.mine), channel_id=1, source_target_pairs={{0,1},{1,0},{2,3},{3,2},{4,5},{5,4},{6,7},{7,6},{8,9},{9,8},{10,11... | collective-permute-start | bytes 983048 | tf_op jit(solution)/shard_map/ppermute | solution.py:374
  66.0 1.7 %collective-permute-start.16 = (bf16[8,32,128]{2,1,0:T(8,128)(2,1)S(1)}, bf16[8,32,128]{2,1,0:T(8,128)(2,1)S(1)}, u32[]{:S(2)}, u32[]{:S(2)}) collective-permute-start(bf16[8,32,128]{2,1,0:T(8,128)(2,1)S(1)} %get-tuple-element.24.refs_0_), channel_id=1, source_target_pairs={{0,1},{1,0},{2,3},{3,2},{4,5},{5,4},{6,7},{7,6},{8,9},{9,8},{10,11... | collective-permute-start | bytes 196616 | tf_op jit(solution)/shard_map/ppermute | solution.py:374
  66.5 1.2 %collective-permute-start.17 = (bf16[8,32,128]{2,1,0:T(8,128)(2,1)S(1)}, bf16[8,32,128]{2,1,0:T(8,128)(2,1)S(1)}, u32[]{:S(2)}, u32[]{:S(2)}) collective-permute-start(bf16[8,32,128]{2,1,0:T(8,128)(2,1)S(1)} %get-tuple-element.24.refs_0_), channel_id=1, source_target_pairs={{1,2},{2,1},{3,4},{4,3},{5,6},{6,5},{7,8},{8,7},{9,10},{10,9},{11,... | collective-permute-start | bytes 196616 | tf_op jit(solution)/shard_map/ppermute | solution.py:374
  69.9 25.1 %copy-start.11 = (f32[2]{0:T(128)S(1)}, f32[2]{0:T(128)}, u32[]{:S(2)}) copy-start(f32[2]{0:T(128)} %weight.1) | copy-start | bytes 28
where the time goes:
time: 97.9 us; the launch traced here: 96.5 us
  waiting for transfers between devices  25 us (26%)
  starting transfers between devices  22.3 us (23%)
  Pallas kernels  21.3 us (22%)
  blocking collectives  18.6 us (19%)
  local copies, waits for them, and re-layouts  8.43 us (9%)
    ppermute x18, waiting for transfers between devices, send(): return lax.ppermute(x, 'clus', pairs)  25 us
    ppermute x18, starting transfers between devices, send(): return lax.ppermute(x, 'clus', pairs)  22.3 us
    all_to_all x1, blocking collectives, shards(): lax.all_to_all(spread, 'clus', 0, 0)  18.6 us
    pallas_call x6, Pallas kernels, near_products(): pl.pallas_call(functools.partial(near_kernel, at, split, fill), out_shape...  12.2 us
    unnamed x36, local copies, waits for them, and re-layouts  8.37 us
    pallas_call x1, Pallas kernels, shards(): pl.pallas_call(inner_kernel, out_shape=(shape((PROBES, 128)), shape((PROB...  2.6 us
    pallas_call x1, Pallas kernels, shards(): pl.pallas_call(image_kernel, out_shape=(shape((OWN, 32, 128)), shape((OWN...  2.26 us
  transfers between devices with their start and end apart: 18, of which 9 were waited for; matrix products, arithmetic and copies ran while one was open for 0% of the time, Pallas kernels for 14%

commit v1 on v0

--- a/solution.py
+++ b/solution.py
@@ -15,11 +15,14 @@
 PROBES = 16
 FMAX = 32
 KMAX = 27
-NEAR_SPLIT = (3, 3, 2)
+FRONT_MIB = 56
+NEAR_MIB = 47
 STAT = 64
 PAY = 80
 VMEM = pl.BlockSpec(memory_space=pltpu.VMEM)
 SMEM = pl.BlockSpec(memory_space=pltpu.SMEM)
+HBM = pl.BlockSpec(memory_space=pltpu.HBM)
+ANY = pl.BlockSpec(memory_space=pl.ANY)
 
 
 def dot_nt(left, right):
@@ -101,22 +104,27 @@
     return jnp.concatenate([column, column], axis=0)
 
 
-def front_kernel(rows, near_list, far_list, probes, col_basis, base, pay, near_at, far_at):
-    me = lax.axis_index("clus")
-    local = near_list[...] - me * OWN
-    flip = (me & 1) * OWN
-    near_at[...] = jnp.where(
-        local < 0, local + 3 * OWN - flip, jnp.where(local < OWN, local, local + flip)
-    )
-    far = far_list[...]
-    owner = far >> 3
-    hop_z = ((me >> 1) - (owner >> 1)) & 3
-    hop_y = ((me >> 3) - (owner >> 3)) & 3
-    place_z = jnp.where(hop_z > 1, 5 - hop_z, hop_z)
-    place_y = jnp.where(hop_y > 1, 5 - hop_y, hop_y)
-    slot = (((me ^ owner) & 1) * 4 + place_y) * 4 + place_z
-    far_at[...] = slot * OWN + (far & 7)
-
+def spread_out(pay, spread, sems):
+    copies = [
+        pltpu.make_async_copy(pay, spread.at[n], sems.at[n]) for n in range(spread.shape[0])
+    ]
+    for copy in copies:
+        copy.start()
+    for copy in copies:
+        copy.wait()
+
+
+def front_kernel(*refs):
+    sources, (base, spread), held, (pay, sems, out_sems) = refs[:3], refs[3:5], refs[5:8], refs[8:]
+    copies = [
+        pltpu.make_async_copy(src, dst, sems.at[n])
+        for n, (src, dst) in enumerate(zip(sources, held))
+    ]
+    for copy in copies:
+        copy.start()
+    rows, probes, col_basis = held
+    for copy in copies:
+        copy.wait()
     lane = lanes(2 * PROBES)
     acc = jnp.zeros((PROBES, 128), F32)
     fields = []
@@ -135,43 +143,79 @@
     pay[0:32] = side_by_side(wide[:4]).astype(BF16)
     pay[32:64] = side_by_side(wide[4:]).astype(BF16)
     pay[STAT:PAY] = three_way(lane_sum(acc), 0).astype(BF16)
-
-
-def pack_kernel(first, coupling, packed):
-    for i in range(packed.shape[0]):
-        for g in range(FMAX // 4):
-            four = [coupling[first + i, 4 * g + f].reshape(2 * RANK, RANK) for f in range(4)]
-            high, low = high_low(jnp.concatenate(four, axis=1))
-            packed[i, :, 128 * g : 128 * g + 128] = jnp.concatenate([high, low], axis=0)
-
-
-def near_kernel(first, split, fill, near_at, near_count, *refs):
-    if fill:
-        own, partner, other, blocks, near, table = refs
-        for group, ref in enumerate((own, partner, other)):
-            for i in range(OWN):
-                field = ref[i].astype(F32)
-                if split:
-                    high, low = high_low(paired(field))
-                    table[OWN * group + i] = jnp.concatenate([high, low], axis=0)
-                else:
-                    table[OWN * group + i] = paired(field).astype(BF16)
+    spread_out(pay, spread, out_sems)
+
+
+def pack_one(coupling, packed, i):
+    for g in range(FMAX // 4):
+        four = [coupling[i, 4 * g + f].reshape(2 * RANK, RANK) for f in range(4)]
+        high, low = high_low(jnp.concatenate(four, axis=1))
+        packed[i, :, 128 * g : 128 * g + 128] = jnp.concatenate([high, low], axis=0)
+
+
+def near_kernel(split, near_list, near_count, *refs):
+    if split:
+        far_list, source, partner, other, blocks, coupling = refs[:6]
+        near, packed, far_at, table, held, sems, kept, more, own, own_sem = refs[6:]
+        fetch = pltpu.make_async_copy(source, own, own_sem)
+        fetch.start()
     else:
-        table, blocks, near = refs
-    count = near.shape[0]
-    acc = [jnp.zeros((128, table.shape[1]), F32) for _ in range(count)]
-    for k in range(KMAX):
-        for i in range(count):
-            vec = table[near_at[first + i, k]]
-            vec = jnp.where(k < near_count[first + i], vec, jnp.zeros_like(vec))
-            mat = jnp.concatenate([blocks[first + i, k, 0], blocks[first + i, k, 1]], axis=1)
-            acc[i] = acc[i] + dot_nt(mat, vec)
-    for i in range(count):
-        out = jnp.transpose(acc[i])
+        own, partner, other, blocks, near, table, held, sems = refs
+    piece = KMAX // 3
+
+    def copy(i, j):
+        span = pl.ds(piece * j, piece)
+        return pltpu.make_async_copy(blocks.at[i, span], held.at[i, span], sems.at[i, j])
+
+    def copy_more(i):
+        return pltpu.make_async_copy(coupling.at[i], kept.at[i], more.at[i])
+
+    for i in range(OWN):
+        for j in range(3):
+            copy(i, j).start()
+    if split:
+        for i in range(OWN):
+            copy_more(i).start()
+    me = lax.axis_index("clus")
+    flip = (me & 1) * OWN
+    if split:
+        far = far_list[...]
+        owner = far >> 3
+        far_at[...] = (((me ^ owner) & 1) * 16 + (owner >> 1)) * OWN + (far & 7)
+        fetch.wait()
+
+    def place(i, k):
+        local = near_list[i, k] - me * OWN
+        return jnp.where(
+            local < 0, local + 3 * OWN - flip, jnp.where(local < OWN, local, local + flip)
+        )
+
+    for group, ref in enumerate((own, partner, other)):
+        for i in range(OWN):
+            field = ref[i].astype(F32)
+            if split:
+                high, low = high_low(paired(field))
+                table[OWN * group + i] = jnp.concatenate([high, low], axis=0)
+            else:
+                table[OWN * group + i] = paired(field).astype(BF16)
+    for i in range(OWN):
+        acc = jnp.zeros((128, table.shape[1]), F32)
+        for j in range(3):
+            copy(i, j).wait()
+            for k in range(piece * j, piece * j + piece):
+                vec = table[place(i, k)]
+                vec = jnp.where(k < near_count[i], vec, jnp.zeros_like(vec))
+                mat = jnp.concatenate([held[i, k, 0], held[i, k, 1]], axis=1)
+                acc = acc + dot_nt(mat, vec)
+        out = jnp.transpose(acc)
         near[i] = out[:32] + out[32:] if split else out
-
-
-def far_fields(far_at, mine, other, packs, row_basis, table, masks):
+    if split:
+        for i in range(OWN):
+            copy_more(i).wait()
+            pack_one(kept, packed, i)
+
+
+def far_fields(far_at, mine, other, packed, row_basis, table, masks):
     for half, ref in enumerate((mine, other)):
         for slot in range(16):
             at = 2 * (16 * half + slot)
@@ -185,8 +229,7 @@
         for f in range(FMAX):
             at = far_at[i, f]
             rows.append(table[at >> 2] * masks[at & 3])
-        packed = packs[i // (OWN // 2)]
-        acc = dot_nn(packed[i % (OWN // 2)], jnp.concatenate(rows, axis=0))
+        acc = dot_nn(packed[i], jnp.concatenate(rows, axis=0))
         folded.append(acc[:64] + acc[64:])
     both = jnp.concatenate(folded, axis=0)
     both = both + pltpu.roll(both, 64, 1)
@@ -210,12 +253,12 @@
 
 
 def image_kernel(far_at, rows, mine, other, *refs):
-    pack_a, pack_b, row_basis, col_basis, *nears, base, image, narrow, pay, keep, table, masks = refs
-    far = far_fields(far_at, mine, other, (pack_a, pack_b), row_basis, table, masks)
+    packed, row_basis, col_basis, near, base, image, narrow, spread, keep = refs[:9]
+    table, masks, pay, out_sems = refs[9:]
+    far = far_fields(far_at, mine, other, packed, row_basis, table, masks)
     beta = jnp.sqrt(column_of(gathered_stat(mine, other), 0, 32, 64) + 1e-06)
     inverse = twice(1.0 / beta)
     lane = lanes(2 * PROBES)
-    near = [ref[i] for ref in nears for i in range(ref.shape[0])]
     acc_re = jnp.zeros((PROBES, 128), F32)
     acc_im = jnp.zeros((PROBES, 128), F32)
     values = []
@@ -235,18 +278,18 @@
     pay[32:64] = side_by_side(wide[4:]).astype(BF16)
     pay[STAT:PAY] = (three_way(lane_sum(acc_re), 0) + three_way(lane_sum(acc_im), 1)).astype(BF16)
     keep[...] = jnp.broadcast_to(beta, (PROBES, 128))
+    spread_out(pay, spread, out_sems)
 
 
 def inner_kernel(far_at, rows, mine, other, *refs):
-    pack_a, pack_b, row_basis, *nears, base, image, keep, sums, head, table, masks = refs
-    far = far_fields(far_at, mine, other, (pack_a, pack_b), row_basis, table, masks)
+    packed, row_basis, near, base, image, keep, sums, head, table, masks = refs
+    far = far_fields(far_at, mine, other, packed, row_basis, table, masks)
     stat = gathered_stat(mine, other)
     hr = column_of(stat, 0, 32, 64)
     hi = column_of(stat, 1, 33, 65)
     beta = column_of(keep[...], 0)
     inverse = twice(1.0 / beta)
     lane = lanes(2 * PROBES)
-    near = [ref[i] for ref in nears for i in range(ref.shape[0])]
 
     def times_h(field):
         re, im = field[:PROBES], field[PROBES:]
@@ -358,32 +401,17 @@
     return pltpu.CompilerParams(vmem_limit_bytes=mib << 20)
 
 
-def z_step(d):
-    return [(i, (i & ~6) | ((((i >> 1) + d) & 3) << 1)) for i in range(32)]
-
-
-def y_step(d):
-    return [(i, (i & 7) | ((((i >> 3) + d) & 3) << 3)) for i in range(32)]
-
-
 CORE = [(i, i ^ 1) for i in range(32)]
-SIDE = [(i, i + 1 if i % 2 else i - 1) for i in range(1, 31)]
+SIDE = [(i, (i + 1 if i % 2 else i - 1) % 32) for i in range(32)]
+COLUMNS = [list(range(k, 32, 2)) for k in range(2)]
 
 
 def send(x, pairs):
     return lax.ppermute(x, "clus", pairs)
 
 
-def gather_ring(x, step):
-    low = send(x, step(1))
-    high = send(x, step(3))
-    last = send(low, step(1))
-    return jnp.concatenate([x, low, high, last], axis=0)
-
-
-def gather_all(pay):
-    four = gather_ring(pay[None], z_step)
-    mine = gather_ring(four, y_step)
+def gather_all(copies):
+    mine = lax.all_to_all(copies, "clus", 0, 0, axis_index_groups=COLUMNS)
     return mine, send(mine, CORE)
 
 
@@ -399,89 +427,90 @@
     far_coupling,
     weight,
 ):
-    base, pay, near_at, far_at = pl.pallas_call(
+    base, spread = pl.pallas_call(
         front_kernel,
-        out_shape=(
-            shape((OWN, 32, 128)),
-            shape((PAY, 128), BF16),
-            shape((OWN, KMAX), jnp.int32),
-            shape((OWN, FMAX), jnp.int32),
-        ),
-        in_specs=[SMEM] + [VMEM] * 4,
-        out_specs=(VMEM,) * 4,
-        compiler_params=params(4),
+        out_shape=(shape((OWN, 32, 128)), shape((16, PAY, 128), BF16)),
+        in_specs=[HBM] * 3,
+        out_specs=(VMEM, ANY),
+        scratch_shapes=[
+            pltpu.SMEM((OWN,), jnp.int32),
+            pltpu.VMEM((OWN, 2, PROBES, 128), F32),
+            pltpu.VMEM((OWN, 2, RANK, 128), BF16),
+            pltpu.VMEM((PAY, 128), BF16),
+            pltpu.SemaphoreType.DMA((3,)),
+            pltpu.SemaphoreType.DMA((16,)),
+        ],
+        compiler_params=params(FRONT_MIB),
         name="front",
-    )(cluster_rows, near_list, far_list, probes, col_basis)
-
-    def pack(first):
-        half = OWN // 2
-        return pl.pallas_call(
-            functools.partial(pack_kernel, first),
-            out_shape=shape((half, 128, 1024), BF16),
-            in_specs=[VMEM],
-            out_specs=VMEM,
-            compiler_params=params(10),
-            cost_estimate=pl.CostEstimate(flops=1 << 20, bytes_accessed=5 << 20, transcendentals=0),
-            name="pack",
-        )(far_coupling)
-
-    def near_products(split, field):
+    )(cluster_rows, probes, col_basis)
+
+    def near_product(split, field):
         partner = send(field, CORE)
         other = send(field, SIDE)
-        height = 64 if split else 32
-        nears, table, at = [], None, 0
-        for part, size in enumerate(NEAR_SPLIT):
-            fill = part == 0
-            out = pl.pallas_call(
-                functools.partial(near_kernel, at, split, fill),
-                out_shape=(shape((size, 32, 128)),)
-                + ((shape((3 * OWN, height, 256), BF16),) if fill else ()),
-                in_specs=[SMEM, SMEM] + [VMEM] * (4 if fill else 2),
-                out_specs=(VMEM,) * (2 if fill else 1),
-                compiler_params=params(16),
-                cost_estimate=pl.CostEstimate(
-                    flops=size * KMAX * 8 * 128 * 128 * 16,
-                    bytes_accessed=size * KMAX << 16,
-                    transcendentals=0,
-                ),
-                name="near",
-            )(near_at, near_count, *((field, partner, other) if fill else (table,)), near_blocks)
-            if fill:
-                table = out[1]
-            nears.append(out[0])
-            at += size
-        return nears
-
-    packs = (pack(0), pack(OWN // 2))
-    nears = near_products(True, base)
-    mine, other = gather_all(pay)
+        blocks_shape = (OWN, KMAX, 2, 128, 128)
+        coupling_shape = (OWN, FMAX, 2, RANK, RANK)
+        out_shape = (shape((OWN, 32, 128)),)
+        scratch = [
+            pltpu.VMEM((3 * OWN, 64 if split else 32, 256), BF16),
+            pltpu.VMEM(blocks_shape, BF16),
+            pltpu.SemaphoreType.DMA((OWN, 3)),
+        ]
+        arguments = (near_list, near_count, field, partner, other, near_blocks)
+        in_specs = [SMEM, SMEM, VMEM, VMEM, VMEM, HBM]
+        if split:
+            out_shape += (shape((OWN, 128, 1024), BF16), shape((OWN, FMAX), jnp.int32))
+            scratch += [
+                pltpu.VMEM(coupling_shape, F32),
+                pltpu.SemaphoreType.DMA((OWN,)),
+                pltpu.VMEM((OWN, 32, 128), F32),
+                pltpu.SemaphoreType.DMA,
+            ]
+            arguments = arguments[:2] + (far_list,) + arguments[2:] + (far_coupling,)
+            in_specs = [SMEM, SMEM, VMEM, ANY, VMEM, VMEM, HBM, HBM]
+        return pl.pallas_call(
+            functools.partial(near_kernel, split),
+            out_shape=out_shape,
+            in_specs=in_specs,
+            out_specs=(VMEM,) * len(out_shape),
+            scratch_shapes=scratch,
+            compiler_params=params(NEAR_MIB),
+            cost_estimate=pl.CostEstimate(
+                flops=OWN * KMAX * 8 * 128 * 128 * 16,
+                bytes_accessed=OWN * KMAX << 16,
+                transcendentals=0,
+            ),
+            name="near",
+        )(*arguments)
+
+    near, packed, far_at = near_product(True, base)
+    mine, other = gather_all(spread)
     scratch = [pltpu.VMEM((64, RANK, 128), BF16), pltpu.VMEM((4, RANK, 128), BF16)]
-    image, narrow, pay_two, keep = pl.pallas_call(
+    image, narrow, spread, keep = pl.pallas_call(
         image_kernel,
         out_shape=(
             shape((OWN, 32, 128)),
             shape((OWN, 32, 128), BF16),
-            shape((PAY, 128), BF16),
+            shape((16, PAY, 128), BF16),
             shape((PROBES, 128)),
         ),
-        in_specs=[SMEM, SMEM] + [VMEM] * (7 + len(nears)),
-        out_specs=(VMEM,) * 4,
-        scratch_shapes=scratch,
+        in_specs=[SMEM, SMEM] + [VMEM] * 7,
+        out_specs=(VMEM, VMEM, ANY, VMEM),
+        scratch_shapes=scratch + [pltpu.VMEM((PAY, 128), BF16), pltpu.SemaphoreType.DMA((16,))],
         compiler_params=params(10),
         name="image",
-    )(far_at, cluster_rows, mine, other, *packs, row_basis, col_basis, *nears, base)
-
-    nears = near_products(False, narrow)
-    mine, other = gather_all(pay_two)
+    )(far_at, cluster_rows, mine, other, packed, row_basis, col_basis, near, base)
+
+    (near,) = near_product(False, narrow)
+    mine, other = gather_all(spread)
     sums, head = pl.pallas_call(
         inner_kernel,
         out_shape=(shape((PROBES, 128)), shape((PROBES, 128))),
-        in_specs=[SMEM, SMEM] + [VMEM] * (8 + len(nears)),
+        in_specs=[SMEM, SMEM] + [VMEM] * 8,
         out_specs=(VMEM, VMEM),
         scratch_shapes=scratch,
         compiler_params=params(10),
         name="inner",
-    )(far_at, cluster_rows, mine, other, *packs, row_basis, *nears, base, image, keep)
+    )(far_at, cluster_rows, mine, other, packed, row_basis, near, base, image, keep)
 
     spread = jnp.broadcast_to(sums[None], (32, PROBES, 128))
     return pl.pallas_call(

time: 97.9 us -> 96.5 us (0.986)
  blocking collectives: 18.6 us -> 41.8 us
  starting transfers between devices: 22.3 us -> 2.82 us
  Pallas kernels: 21.3 us -> 34.4 us
  waiting for transfers between devices: 25 us -> 12.1 us
  local copies, waits for them, and re-layouts: 8.43 us -> 2.99 us
    all_to_all x0 -> x2, blocking collectives: none -> 29.9 us  [gather_all(): mine = lax.all_to_all(copies, 'clus', 0, 0, axis_index_groups=COLUMNS)]
    ppermute x18 -> x6, starting transfers between devices: 22.3 us -> 2.82 us  [send(): return lax.ppermute(x, 'clus', pairs)]
    ppermute x18 -> x6, waiting for transfers between devices: 25 us -> 12.1 us  [send(): return lax.ppermute(x, 'clus', pairs)]
    pallas_call x9 -> x3, Pallas kernels: 14.9 us -> 27.2 us  [the longest x2 24.3 us: near_product(): pl.pallas_call(functools.partial(near_kernel, split), out_shape=out_shape...]
    all_to_all x1, blocking collectives: 18.6 us -> 11.9 us  [shards(): lax.all_to_all(spread, 'clus', 0, 0)]
    unnamed x36 -> x18, local copies, waits for them, and re-layouts: 8.37 us -> 2.96 us
  transfers between devices with their start and end apart: 18 -> 6, of which waited for: 9 -> 2; matrix products, arithmetic and copies ran while one was open for 0% -> 0% of each run, Pallas kernels for 14% -> 26%
where the time goes in v1:
time: 96.5 us; the launch traced here: 94.9 us
  blocking collectives  41.8 us (43%)
  Pallas kernels  34.4 us (36%)
  waiting for transfers between devices  12.1 us (13%)
  local copies, waits for them, and re-layouts  2.99 us (3%)
  starting transfers between devices  2.82 us (3%)
    all_to_all x2, blocking collectives, gather_all(): mine = lax.all_to_all(copies, 'clus', 0, 0, axis_index_groups=COLUMNS)  29.9 us
    pallas_call x2, Pallas kernels, near_product(): pl.pallas_call(functools.partial(near_kernel, split), out_shape=out_shape...  24.3 us
    ppermute x6, waiting for transfers between devices, send(): return lax.ppermute(x, 'clus', pairs)  12.1 us
    all_to_all x1, blocking collectives, shards(): lax.all_to_all(spread, 'clus', 0, 0)  11.9 us
    pallas_call x1, Pallas kernels, shards(): pl.pallas_call(front_kernel, out_shape=(shape((OWN, 32, 128)), shape((16,...  2.99 us
    pallas_call x1, Pallas kernels, shards(): pl.pallas_call(image_kernel, out_shape=(shape((OWN, 32, 128)), shape((OWN...  2.98 us
    unnamed x18, local copies, waits for them, and re-layouts  2.96 us
    ppermute x6, starting transfers between devices, send(): return lax.ppermute(x, 'clus', pairs)  2.82 us
  transfers between devices with their start and end apart: 6, of which 2 were waited for; matrix products, arithmetic and copies ran while one was open for 0% of the time, Pallas kernels for 26%

profile of v1, /device:TPU:0, one launch (start us, length us, event | category | flops | bytes accessed | tf_op | source)
XLA Modules:
  0.0 94.9 jit_solution(4590108628138595175)
XLA Ops:
  0.6 3.0 %front.1 = (f32[8,32,128]{2,1,0:T(8,128)}, bf16[16,80,128]{2,1,0:T(8,128)(2,1)}) custom-call(s32[8]{0:T(128)} %rows.3, f32[8,2,16,128]{3,2,1,0:T(8,128)} %refs_1_.3, bf16[8,2,32,128]{3,2,1,0:T(8,128)(2,1)} %refs_2_.3), custom_call_target="tpu_custom_call" | custom-call | tf_op jit(solution)/shard_map/front/pallas_call | solution.py:430
  3.6 0.0 copy-start.2
  3.6 0.0 copy-start.3
  3.6 17.5 %all_to_all.15.mine = bf16[16,80,128]{2,1,0:T(8,128)(2,1)S(1)} all-to-all(bf16[16,80,128]{2,1,0:T(8,128)(2,1)} %get-tuple-element.16), channel_id=1, replica_groups={{0,2,4,6,8,10,12,14,16,18,20,22,24,26,28,30},{1,3,5,7,9,11,13,15,17,19,..., dimensions={0} | all-to-all | bytes 655360 | tf_op jit(solution)/shard_map/all_to_all | solution.py:414
  21.1 0.0 collective-permute-start.2
  21.1 1.4 %collective-permute-start.1 = (f32[8,32,128]{2,1,0:T(8,128)}, f32[8,32,128]{2,1,0:T(8,128)S(1)}, u32[]{:S(2)}, u32[]{:S(2)}) collective-permute-start(f32[8,32,128]{2,1,0:T(8,128)} %get-tuple-element.14.refs_1_.refs_4_.refs_3_.base), channel_id=1, source_target_pairs={{0,31},{1,2},{2,1},{3,4},{4,3},{5,6},{6,5},{7,8},{8,7},{9,10},{10,... | collective-permute-start | bytes 393224 | tf_op jit(solution)/shard_map/ppermute | solution.py:410
  22.5 0.0 collective-permute-start
  22.5 6.5 %collective-permute-done.1.refs_3_ = f32[8,32,128]{2,1,0:T(8,128)S(1)} collective-permute-done((f32[8,32,128]{2,1,0:T(8,128)}, f32[8,32,128]{2,1,0:T(8,128)S(1)}, u32[]{:S(2)}, u32[]{:S(2)}) %collective-permute-start.1) | collective-permute-done | bytes 131104 | tf_op jit(solution)/shard_map/ppermute | solution.py:410
  29.0 0.0 collective-permute-done.refs_2_
  29.0 0.9 copy-done
  30.0 0.7 copy-done.4
  30.6 0.7 copy-done.6
  31.3 0.7 copy-done.7
  32.0 13.5 %near.2 = (f32[8,32,128]{2,1,0:T(8,128)S(1)}, bf16[8,128,1024]{2,1,0:T(8,128)(2,1)S(1)}, s32[8,32]{1,0:T(8,128)S(1)}) custom-call(s32[8,27]{1,0:T(8,128)S(1)} %copy-done.4, s32[8]{0:T(128)S(1)} %copy-done.7, s32[8,32]{1,0:T(8,128)S(1)} %copy-done.6, f32[8,32,128]{2,1,0:T(8,128)S(1)} %copy-done, f32[8,32,128]{2,1,0:T(8,128)S(1)} %collective-permute-done.refs_2_, ...), custom_call_target="tpu_custom_call" | custom-call | flops 452984832 | bytes 14155776 | tf_op jit(solution)/shard_map/near/pallas_call | solution.py:470
  45.5 0.0 collective-permute-done.2.other
  45.5 0.0 copy-done.2
  45.5 0.0 copy-done.3
  45.5 0.0 copy-done.5
  45.5 3.0 %image.1 = (f32[8,32,128]{2,1,0:T(8,128)S(1)}, bf16[8,32,128]{2,1,0:T(8,128)(2,1)S(1)}, bf16[16,80,128]{2,1,0:T(8,128)(2,1)S(1)}, f32[16,128]{1,0:T(8,128)S(1)}) custom-call(s32[8,32]{1,0:T(8,128)S(1)} %get-tuple-element.15.far_at, s32[8]{0:T(128)S(1)} %copy-done.5, bf16[16,80,128]{2,1,0:T(8,128)(2,1)S(1)} %all_to_all.15.mine, ...), custom_call_target="tpu_custom_call" | custom-call | tf_op jit(solution)/shard_map/image/pallas_call | solution.py:488
  48.5 0.0 copy-start.1
  48.5 12.4 %all_to_all.16.mine = bf16[16,80,128]{2,1,0:T(8,128)(2,1)S(1)} all-to-all(bf16[16,80,128]{2,1,0:T(8,128)(2,1)S(1)} %get-tuple-element.19), channel_id=1, replica_groups={{0,2,4,6,8,10,12,14,16,18,20,22,24,26,28,30},{1,3,5,7,9,11,13,15,17,19,..., dimensions={0} | all-to-all | bytes 655360 | tf_op jit(solution)/shard_map/all_to_all | solution.py:414
  61.0 0.0 collective-permute-start.3
  61.0 1.4 %collective-permute-start.5 = (bf16[8,32,128]{2,1,0:T(8,128)(2,1)S(1)}, bf16[8,32,128]{2,1,0:T(8,128)(2,1)S(1)}, u32[]{:S(2)}, u32[]{:S(2)}) collective-permute-start(bf16[8,32,128]{2,1,0:T(8,128)(2,1)S(1)} %get-tuple-element.20.refs_0_), channel_id=1, source_target_pairs={{0,31},{1,2},{2,1},{3,4},{4,3},{5,6},{6,5},{7,8},{8,7},{9,10},{10,... | collective-permute-start | bytes 196616 | tf_op jit(solution)/shard_map/ppermute | solution.py:410
  62.4 0.0 collective-permute-start.4
  62.4 5.6 %collective-permute-done.5.refs_2_ = bf16[8,32,128]{2,1,0:T(8,128)(2,1)S(1)} collective-permute-done((bf16[8,32,128]{2,1,0:T(8,128)(2,1)S(1)}, bf16[8,32,128]{2,1,0:T(8,128)(2,1)S(1)}, u32[]{:S(2)}, u32[]{:S(2)}) %collective-permute-start.5) | collective-permute-done | bytes 65568 | tf_op jit(solution)/shard_map/ppermute | solution.py:410
  68.0 0.0 collective-permute-done.4.refs_1_
  68.0 10.8 %near.3.refs_2_ = f32[8,32,128]{2,1,0:T(8,128)S(1)} custom-call(s32[8,27]{1,0:T(8,128)S(1)} %copy-done.4, s32[8]{0:T(128)S(1)} %copy-done.7, bf16[8,32,128]{2,1,0:T(8,128)(2,1)S(1)} %get-tuple-element.20.refs_0_, bf16[8,32,128]{2,1,0:T(8,128)(2,1)S(1)} %collective-permute-done.4.refs_1_, bf16[8,32,128]{2,1,0:T(8,128)(2,1)S(1)} %collective-permute-done.5.refs_2_, ...), custom_call_target="tpu_custom_call" | custom-call | flops 452984832 | bytes 14155776 | tf_op jit(solution)/shard_map/near/pallas_call | solution.py:470
  78.8 0.0 collective-permute-done.3.other
  78.8 2.6 %inner.1 = (f32[16,128]{1,0:T(8,128)S(1)}, f32[16,128]{1,0:T(8,128)S(1)}) custom-call(s32[8,32]{1,0:T(8,128)S(1)} %get-tuple-element.15.far_at, s32[8]{0:T(128)S(1)} %copy-done.5, bf16[16,80,128]{2,1,0:T(8,128)(2,1)S(1)} %all_to_all.16.mine, bf16[16,80,128]{2,1,0:T(8,128)(2,1)S(1)} %collective-permute-done.3.other, ...), custom_call_target="tpu_custom_call" | custom-call | tf_op jit(solution)/shard_map/inner/pallas_call | solution.py:505
  81.5 11.9 %all_to_all.17.sums = f32[32,16,128]{2,1,0:T(8,128)S(1)} all-to-all(f32[32,16,128]{2,1,0:T(8,128)S(1)} %broadcast_in_dim.2), channel_id=1, replica_groups=mesh['contour'=4,'clus'=32] {'clus'}, dimensions={0} | all-to-all | bytes 524288 | tf_op jit(solution)/shard_map/all_to_all | solution.py:523
  93.4 0.0 copy-done.8
  93.4 1.5 %final.1 = (f32[8,2,16,128]{3,2,1,0:T(8,128)}, f32[2,16,16]{2,1,0:T(8,128)}, f32[4,16]{1,0:T(4,128)}) custom-call(f32[2]{0:T(128)S(1)} %copy-done.8, f32[32,16,128]{2,1,0:T(8,128)S(1)} %all_to_all.17.sums, f32[16,128]{1,0:T(8,128)S(1)} %get-tuple-element.24.head, f32[8,32,128]{2,1,0:T(8,128)S(1)} %copy-done.1, f32[8,32,128]{2,1,0:T(8,128)S(1)} %get-tuple-element.21.refs_4_.image), custom_call_target="tpu_custom_call" | custom-call | tf_op jit(solution)/shard_map/final/pallas_call | solution.py:516
  (8 shorter events, 0.0 us)
Async XLA Ops:
  3.6 41.9 %copy-start.2 = (bf16[8,2,32,128]{3,2,1,0:T(8,128)(2,1)S(1)}, bf16[8,2,32,128]{3,2,1,0:T(8,128)(2,1)}, u32[]{:S(2)}) copy-start(bf16[8,2,32,128]{3,2,1,0:T(8,128)(2,1)} %refs_1_.5) | copy-start | bytes 393220
  3.6 41.9 %copy-start.3 = (bf16[8,2,32,128]{3,2,1,0:T(8,128)(2,1)S(1)}, bf16[8,2,32,128]{3,2,1,0:T(8,128)(2,1)}, u32[]{:S(2)}) copy-start(bf16[8,2,32,128]{3,2,1,0:T(8,128)(2,1)} %refs_2_.3) | copy-start | bytes 393220
  21.1 24.4 %collective-permute-start.2 = (bf16[16,80,128]{2,1,0:T(8,128)(2,1)S(1)}, bf16[16,80,128]{2,1,0:T(8,128)(2,1)S(1)}, u32[]{:S(2)}, u32[]{:S(2)}) collective-permute-start(bf16[16,80,128]{2,1,0:T(8,128)(2,1)S(1)} %all_to_all.15.mine), channel_id=1, source_target_pairs={{0,1},{1,0},{2,3},{3,2},{4,5},{5,4},{6,7},{7,6},{8,9},{9,8},{10,11... | collective-permute-start | bytes 983048 | tf_op jit(solution)/shard_map/ppermute | solution.py:410
  21.1 24.4 %copy-start.5 = (s32[8]{0:T(128)S(1)}, s32[8]{0:T(128)}, u32[]{:S(2)}) copy-start(s32[8]{0:T(128)} %rows.3) | copy-start | bytes 100
  21.1 7.9 %collective-permute-start.1 = (f32[8,32,128]{2,1,0:T(8,128)}, f32[8,32,128]{2,1,0:T(8,128)S(1)}, u32[]{:S(2)}, u32[]{:S(2)}) collective-permute-start(f32[8,32,128]{2,1,0:T(8,128)} %get-tuple-element.14.refs_1_.refs_4_.refs_3_.base), channel_id=1, source_target_pairs={{0,31},{1,2},{2,1},{3,4},{4,3},{5,6},{6,5},{7,8},{8,7},{9,10},{10,... | collective-permute-start | bytes 393224 | tf_op jit(solution)/shard_map/ppermute | solution.py:410
  22.5 6.5 %collective-permute-start = (f32[8,32,128]{2,1,0:T(8,128)}, f32[8,32,128]{2,1,0:T(8,128)S(1)}, u32[]{:S(2)}, u32[]{:S(2)}) collective-permute-start(f32[8,32,128]{2,1,0:T(8,128)} %get-tuple-element.14.refs_1_.refs_4_.refs_3_.base), channel_id=1, source_target_pairs={{0,1},{1,0},{2,3},{3,2},{4,5},{5,4},{6,7},{7,6},{8,9},{9,8},{10,11... | collective-permute-start | bytes 393224 | tf_op jit(solution)/shard_map/ppermute | solution.py:410
  29.0 0.9 copy-start
  30.0 0.7 copy-start.4
  30.6 0.7 copy-start.6
  31.3 0.7 copy-start.7
  48.5 30.3 %copy-start.1 = (f32[8,32,128]{2,1,0:T(8,128)S(1)}, f32[8,32,128]{2,1,0:T(8,128)}, u32[]{:S(2)}) copy-start(f32[8,32,128]{2,1,0:T(8,128)} %get-tuple-element.14.refs_1_.refs_4_.refs_3_.base) | copy-start | bytes 393220
  61.0 17.8 %collective-permute-start.3 = (bf16[16,80,128]{2,1,0:T(8,128)(2,1)S(1)}, bf16[16,80,128]{2,1,0:T(8,128)(2,1)S(1)}, u32[]{:S(2)}, u32[]{:S(2)}) collective-permute-start(bf16[16,80,128]{2,1,0:T(8,128)(2,1)S(1)} %all_to_all.16.mine), channel_id=1, source_target_pairs={{0,1},{1,0},{2,3},{3,2},{4,5},{5,4},{6,7},{7,6},{8,9},{9,8},{10,11... | collective-permute-start | bytes 983048 | tf_op jit(solution)/shard_map/ppermute | solution.py:410
  61.0 32.4 %copy-start.8 = (f32[2]{0:T(128)S(1)}, f32[2]{0:T(128)}, u32[]{:S(2)}) copy-start(f32[2]{0:T(128)} %weight.1) | copy-start | bytes 28
  61.0 7.0 %collective-permute-start.5 = (bf16[8,32,128]{2,1,0:T(8,128)(2,1)S(1)}, bf16[8,32,128]{2,1,0:T(8,128)(2,1)S(1)}, u32[]{:S(2)}, u32[]{:S(2)}) collective-permute-start(bf16[8,32,128]{2,1,0:T(8,128)(2,1)S(1)} %get-tuple-element.20.refs_0_), channel_id=1, source_target_pairs={{0,31},{1,2},{2,1},{3,4},{4,3},{5,6},{6,5},{7,8},{8,7},{9,10},{10,... | collective-permute-start | bytes 196616 | tf_op jit(solution)/shard_map/ppermute | solution.py:410
  62.4 5.6 %collective-permute-start.4 = (bf16[8,32,128]{2,1,0:T(8,128)(2,1)S(1)}, bf16[8,32,128]{2,1,0:T(8,128)(2,1)S(1)}, u32[]{:S(2)}, u32[]{:S(2)}) collective-permute-start(bf16[8,32,128]{2,1,0:T(8,128)(2,1)S(1)} %get-tuple-element.20.refs_0_), channel_id=1, source_target_pairs={{0,1},{1,0},{2,3},{3,2},{4,5},{5,4},{6,7},{7,6},{8,9},{9,8},{10,11... | collective-permute-start | bytes 196616 | tf_op jit(solution)/shard_map/ppermute | solution.py:410

commit v2 on v1

--- a/solution.py
+++ b/solution.py
@@ -15,7 +15,9 @@
 PROBES = 16
 FMAX = 32
 KMAX = 27
-FRONT_MIB = 56
+FRONT_MIB = 2
+PIECES = ((0, 1), (1, 2), (3, 2), (5, 3))
+PACK_PIECES = ((0, 4), (4, 2), (6, 2))
 NEAR_MIB = 47
 STAT = 64
 PAY = 80
@@ -114,17 +116,7 @@
         copy.wait()
 
 
-def front_kernel(*refs):
-    sources, (base, spread), held, (pay, sems, out_sems) = refs[:3], refs[3:5], refs[5:8], refs[8:]
-    copies = [
-        pltpu.make_async_copy(src, dst, sems.at[n])
-        for n, (src, dst) in enumerate(zip(sources, held))
-    ]
-    for copy in copies:
-        copy.start()
-    rows, probes, col_basis = held
-    for copy in copies:
-        copy.wait()
+def front_kernel(rows, probes, col_basis, base, spread, pay, out_sems):
     lane = lanes(2 * PROBES)
     acc = jnp.zeros((PROBES, 128), F32)
     fields = []
@@ -155,34 +147,32 @@
 
 def near_kernel(split, near_list, near_count, *refs):
     if split:
-        far_list, source, partner, other, blocks, coupling = refs[:6]
-        near, packed, far_at, table, held, sems, kept, more, own, own_sem = refs[6:]
-        fetch = pltpu.make_async_copy(source, own, own_sem)
-        fetch.start()
+        far_list, own, partner, other, blocks, coupling, near, packed, far_at = refs[:9]
+        table, held, sems, kept, more = refs[9:]
     else:
         own, partner, other, blocks, near, table, held, sems = refs
-    piece = KMAX // 3
-
-    def copy(i, j):
-        span = pl.ds(piece * j, piece)
-        return pltpu.make_async_copy(blocks.at[i, span], held.at[i, span], sems.at[i, j])
-
-    def copy_more(i):
-        return pltpu.make_async_copy(coupling.at[i], kept.at[i], more.at[i])
-
-    for i in range(OWN):
-        for j in range(3):
-            copy(i, j).start()
-    if split:
-        for i in range(OWN):
-            copy_more(i).start()
+    pieces = [
+        pltpu.make_async_copy(
+            blocks.at[pl.ds(at, size)], held.at[pl.ds(at, size)], sems.at[n]
+        )
+        for n, (at, size) in enumerate(PIECES)
+    ]
+    for piece in pieces:
+        piece.start()
     me = lax.axis_index("clus")
     flip = (me & 1) * OWN
     if split:
+        late = [
+            pltpu.make_async_copy(
+                coupling.at[pl.ds(at, size)], kept.at[pl.ds(at, size)], more.at[n]
+            )
+            for n, (at, size) in enumerate(PACK_PIECES)
+        ]
+        for piece in late:
+            piece.start()
         far = far_list[...]
         owner = far >> 3
         far_at[...] = (((me ^ owner) & 1) * 16 + (owner >> 1)) * OWN + (far & 7)
-        fetch.wait()
 
     def place(i, k):
         local = near_list[i, k] - me * OWN
@@ -198,21 +188,23 @@
                 table[OWN * group + i] = jnp.concatenate([high, low], axis=0)
             else:
                 table[OWN * group + i] = paired(field).astype(BF16)
-    for i in range(OWN):
-        acc = jnp.zeros((128, table.shape[1]), F32)
-        for j in range(3):
-            copy(i, j).wait()
-            for k in range(piece * j, piece * j + piece):
-                vec = table[place(i, k)]
-                vec = jnp.where(k < near_count[i], vec, jnp.zeros_like(vec))
-                mat = jnp.concatenate([held[i, k, 0], held[i, k, 1]], axis=1)
-                acc = acc + dot_nt(mat, vec)
-        out = jnp.transpose(acc)
-        near[i] = out[:32] + out[32:] if split else out
+    for (at, size), piece in zip(PIECES, pieces):
+        piece.wait()
+        acc = [jnp.zeros((128, table.shape[1]), F32) for _ in range(size)]
+        for k in range(KMAX):
+            for j in range(size):
+                vec = table[place(at + j, k)]
+                vec = jnp.where(k < near_count[at + j], vec, jnp.zeros_like(vec))
+                mat = jnp.concatenate([held[at + j, k, 0], held[at + j, k, 1]], axis=1)
+                acc[j] = acc[j] + dot_nt(mat, vec)
+        for j in range(size):
+            out = jnp.transpose(acc[j])
+            near[at + j] = out[:32] + out[32:] if split else out
     if split:
-        for i in range(OWN):
-            copy_more(i).wait()
-            pack_one(kept, packed, i)
+        for (at, size), piece in zip(PACK_PIECES, late):
+            piece.wait()
+            for i in range(at, at + size):
+                pack_one(kept, packed, i)
 
 
 def far_fields(far_at, mine, other, packed, row_basis, table, masks):
@@ -253,8 +245,8 @@
 
 
 def image_kernel(far_at, rows, mine, other, *refs):
-    packed, row_basis, col_basis, near, base, image, narrow, spread, keep = refs[:9]
-    table, masks, pay, out_sems = refs[9:]
+    packed, row_basis, col_basis, near, base, image, narrow, spread, keep = refs[:-4]
+    table, masks, pay, out_sems = refs[-4:]
     far = far_fields(far_at, mine, other, packed, row_basis, table, masks)
     beta = jnp.sqrt(column_of(gathered_stat(mine, other), 0, 32, 64) + 1e-06)
     inverse = twice(1.0 / beta)
@@ -430,16 +422,9 @@
     base, spread = pl.pallas_call(
         front_kernel,
         out_shape=(shape((OWN, 32, 128)), shape((16, PAY, 128), BF16)),
-        in_specs=[HBM] * 3,
+        in_specs=[SMEM, VMEM, VMEM],
         out_specs=(VMEM, ANY),
-        scratch_shapes=[
-            pltpu.SMEM((OWN,), jnp.int32),
-            pltpu.VMEM((OWN, 2, PROBES, 128), F32),
-            pltpu.VMEM((OWN, 2, RANK, 128), BF16),
-            pltpu.VMEM((PAY, 128), BF16),
-            pltpu.SemaphoreType.DMA((3,)),
-            pltpu.SemaphoreType.DMA((16,)),
-        ],
+        scratch_shapes=[pltpu.VMEM((PAY, 128), BF16), pltpu.SemaphoreType.DMA((16,))],
         compiler_params=params(FRONT_MIB),
         name="front",
     )(cluster_rows, probes, col_basis)
@@ -447,31 +432,27 @@
     def near_product(split, field):
         partner = send(field, CORE)
         other = send(field, SIDE)
-        blocks_shape = (OWN, KMAX, 2, 128, 128)
-        coupling_shape = (OWN, FMAX, 2, RANK, RANK)
-        out_shape = (shape((OWN, 32, 128)),)
+        out_shape = [shape((OWN, 32, 128))]
         scratch = [
             pltpu.VMEM((3 * OWN, 64 if split else 32, 256), BF16),
-            pltpu.VMEM(blocks_shape, BF16),
-            pltpu.SemaphoreType.DMA((OWN, 3)),
+            pltpu.VMEM((OWN, KMAX, 2, 128, 128), BF16),
+            pltpu.SemaphoreType.DMA((len(PIECES),)),
         ]
-        arguments = (near_list, near_count, field, partner, other, near_blocks)
-        in_specs = [SMEM, SMEM, VMEM, VMEM, VMEM, HBM]
+        arguments = [field, partner, other, near_blocks]
+        in_specs = [VMEM, VMEM, VMEM, HBM]
         if split:
-            out_shape += (shape((OWN, 128, 1024), BF16), shape((OWN, FMAX), jnp.int32))
+            out_shape += [shape((OWN, 128, 1024), BF16), shape((OWN, FMAX), jnp.int32)]
             scratch += [
-                pltpu.VMEM(coupling_shape, F32),
-                pltpu.SemaphoreType.DMA((OWN,)),
-                pltpu.VMEM((OWN, 32, 128), F32),
-                pltpu.SemaphoreType.DMA,
+                pltpu.VMEM((OWN, FMAX, 2, RANK, RANK), F32),
+                pltpu.SemaphoreType.DMA((len(PACK_PIECES),)),
             ]
-            arguments = arguments[:2] + (far_list,) + arguments[2:] + (far_coupling,)
-            in_specs = [SMEM, SMEM, VMEM, ANY, VMEM, VMEM, HBM, HBM]
+            arguments = [far_list] + arguments + [far_coupling]
+            in_specs = [VMEM] + in_specs + [HBM]
         return pl.pallas_call(
             functools.partial(near_kernel, split),
             out_shape=out_shape,
-            in_specs=in_specs,
-            out_specs=(VMEM,) * len(out_shape),
+            in_specs=[SMEM, SMEM] + in_specs,
+            out_specs=[VMEM] * len(out_shape),
             scratch_shapes=scratch,
             compiler_params=params(NEAR_MIB),
             cost_estimate=pl.CostEstimate(
@@ -480,7 +461,7 @@
                 transcendentals=0,
             ),
             name="near",
-        )(*arguments)
+        )(near_list, near_count, *arguments)
 
     near, packed, far_at = near_product(True, base)
     mine, other = gather_all(spread)

time: 96.5 us -> 93.1 us (0.965)
  Pallas kernels: 34.4 us -> 30.3 us
  local copies, waits for them, and re-layouts: 2.99 us -> 4.53 us
    pallas_call x2, Pallas kernels: 24.3 us -> 21.5 us  [near_product(): pl.pallas_call(functools.partial(near_kernel, split), out_shape=out_shape...]
    unnamed x18 -> x20, local copies, waits for them, and re-layouts: 2.96 us -> 4.5 us
    pallas_call x1, Pallas kernels: 2.99 us -> 1.6 us  [shards(): pl.pallas_call(front_kernel, out_shape=(shape((OWN, 32, 128)), shape((16,...]
  transfers between devices with their start and end apart: 6 -> 6, of which waited for: 2 -> 2; matrix products, arithmetic and copies ran while one was open for 0% -> 0% of each run, Pallas kernels for 26% -> 23%
where the time goes in v2:
time: 93.1 us; the launch traced here: 91.6 us
  blocking collectives  41.2 us (44%)
  Pallas kernels  30.3 us (33%)
  waiting for transfers between devices  12 us (13%)
  local copies, waits for them, and re-layouts  4.53 us (5%)
  starting transfers between devices  2.82 us (3%)
    all_to_all x2, blocking collectives, gather_all(): mine = lax.all_to_all(copies, 'clus', 0, 0, axis_index_groups=COLUMNS)  29.3 us
    pallas_call x2, Pallas kernels, near_product(): pl.pallas_call(functools.partial(near_kernel, split), out_shape=out_shape...  21.5 us
    ppermute x6, waiting for transfers between devices, send(): return lax.ppermute(x, 'clus', pairs)  12 us
    all_to_all x1, blocking collectives, shards(): lax.all_to_all(spread, 'clus', 0, 0)  11.9 us
    unnamed x20, local copies, waits for them, and re-layouts  4.5 us
    pallas_call x1, Pallas kernels, shards(): pl.pallas_call(image_kernel, out_shape=(shape((OWN, 32, 128)), shape((OWN...  2.98 us
    ppermute x6, starting transfers between devices, send(): return lax.ppermute(x, 'clus', pairs)  2.82 us
    pallas_call x1, Pallas kernels, shards(): pl.pallas_call(inner_kernel, out_shape=(shape((PROBES, 128)), shape((PROB...  2.64 us
  transfers between devices with their start and end apart: 6, of which 2 were waited for; matrix products, arithmetic and copies ran while one was open for 0% of the time, Pallas kernels for 23%

profile of v2, /device:TPU:0, one launch (start us, length us, event | category | flops | bytes accessed | tf_op | source)
XLA Modules:
  0.0 91.6 jit_solution(10379545474022523475)
XLA Ops:
  0.6 0.0 copy-start.1
  0.6 0.9 copy-done.1
  1.5 0.9 copy-done.3
  2.4 0.7 copy-done.5
  3.1 1.6 %front.1 = (f32[8,32,128]{2,1,0:T(8,128)S(1)}, bf16[16,80,128]{2,1,0:T(8,128)(2,1)S(1)}) custom-call(s32[8]{0:T(128)S(1)} %copy-done.5, f32[8,2,16,128]{3,2,1,0:T(8,128)S(1)} %copy-done.3, bf16[8,2,32,128]{3,2,1,0:T(8,128)(2,1)S(1)} %copy-done.1), custom_call_target="tpu_custom_call" | custom-call | tf_op jit(solution)/shard_map/front/pallas_call | solution.py:422
  4.7 17.1 %all_to_all.15.mine = bf16[16,80,128]{2,1,0:T(8,128)(2,1)S(1)} all-to-all(bf16[16,80,128]{2,1,0:T(8,128)(2,1)S(1)} %get-tuple-element.16), channel_id=1, replica_groups={{0,2,4,6,8,10,12,14,16,18,20,22,24,26,28,30},{1,3,5,7,9,11,13,15,17,19,..., dimensions={0} | all-to-all | bytes 655360 | tf_op jit(solution)/shard_map/all_to_all | solution.py:406
  21.8 0.0 collective-permute-start.2
  21.8 1.4 %collective-permute-start.1 = (f32[8,32,128]{2,1,0:T(8,128)S(1)}, f32[8,32,128]{2,1,0:T(8,128)S(1)}, u32[]{:S(2)}, u32[]{:S(2)}) collective-permute-start(f32[8,32,128]{2,1,0:T(8,128)S(1)} %get-tuple-element.14.refs_1_.refs_4_.refs_3_.base), channel_id=1, source_target_pairs={{0,31},{1,2},{2,1},{3,4},{4,3},{5,6},{6,5},{7,8},{8,7},{9,10},{10,... | collective-permute-start | bytes 393224 | tf_op jit(solution)/shard_map/ppermute | solution.py:402
  23.2 0.0 collective-permute-start
  23.2 6.4 %collective-permute-done.1.refs_3_ = f32[8,32,128]{2,1,0:T(8,128)S(1)} collective-permute-done((f32[8,32,128]{2,1,0:T(8,128)S(1)}, f32[8,32,128]{2,1,0:T(8,128)S(1)}, u32[]{:S(2)}, u32[]{:S(2)}) %collective-permute-start.1) | collective-permute-done | bytes 131104 | tf_op jit(solution)/shard_map/ppermute | solution.py:402
  29.6 0.0 collective-permute-done.refs_2_
  29.6 0.7 copy-done.4
  30.3 0.7 copy-done.7
  31.0 0.7 copy-done.8
  31.7 12.3 %near.2 = (f32[8,32,128]{2,1,0:T(8,128)S(1)}, bf16[8,128,1024]{2,1,0:T(8,128)(2,1)S(1)}, s32[8,32]{1,0:T(8,128)S(1)}) custom-call(s32[8,27]{1,0:T(8,128)S(1)} %copy-done.4, s32[8]{0:T(128)S(1)} %copy-done.8, s32[8,32]{1,0:T(8,128)S(1)} %copy-done.7, f32[8,32,128]{2,1,0:T(8,128)S(1)} %get-tuple-element.14.refs_1_.refs_4_.refs_3_.base, ...), custom_call_target="tpu_custom_call" | custom-call | flops 452984832 | bytes 14155776 | tf_op jit(solution)/shard_map/near/pallas_call | solution.py:451
  44.0 0.0 collective-permute-done.2.other
  44.0 0.0 copy-done.6
  44.0 0.0 copy-done
  44.0 0.0 copy-done.2
  44.0 3.0 %image.1 = (f32[8,32,128]{2,1,0:T(8,128)S(1)}, bf16[8,32,128]{2,1,0:T(8,128)(2,1)S(1)}, bf16[16,80,128]{2,1,0:T(8,128)(2,1)S(1)}, f32[16,128]{1,0:T(8,128)S(1)}) custom-call(s32[8,32]{1,0:T(8,128)S(1)} %get-tuple-element.15.far_at, s32[8]{0:T(128)S(1)} %copy-done.6, bf16[16,80,128]{2,1,0:T(8,128)(2,1)S(1)} %all_to_all.15.mine, ...), custom_call_target="tpu_custom_call" | custom-call | tf_op jit(solution)/shard_map/image/pallas_call | solution.py:469
  47.0 12.2 %all_to_all.16.mine = bf16[16,80,128]{2,1,0:T(8,128)(2,1)S(1)} all-to-all(bf16[16,80,128]{2,1,0:T(8,128)(2,1)S(1)} %get-tuple-element.19), channel_id=1, replica_groups={{0,2,4,6,8,10,12,14,16,18,20,22,24,26,28,30},{1,3,5,7,9,11,13,15,17,19,..., dimensions={0} | all-to-all | bytes 655360 | tf_op jit(solution)/shard_map/all_to_all | solution.py:406
  59.3 0.0 collective-permute-start.3
  59.3 1.4 %collective-permute-start.5 = (bf16[8,32,128]{2,1,0:T(8,128)(2,1)S(1)}, bf16[8,32,128]{2,1,0:T(8,128)(2,1)S(1)}, u32[]{:S(2)}, u32[]{:S(2)}) collective-permute-start(bf16[8,32,128]{2,1,0:T(8,128)(2,1)S(1)} %get-tuple-element.20.refs_0_), channel_id=1, source_target_pairs={{0,31},{1,2},{2,1},{3,4},{4,3},{5,6},{6,5},{7,8},{8,7},{9,10},{10,... | collective-permute-start | bytes 196616 | tf_op jit(solution)/shard_map/ppermute | solution.py:402
  60.7 0.0 collective-permute-start.4
  60.7 5.6 %collective-permute-done.5.refs_2_ = bf16[8,32,128]{2,1,0:T(8,128)(2,1)S(1)} collective-permute-done((bf16[8,32,128]{2,1,0:T(8,128)(2,1)S(1)}, bf16[8,32,128]{2,1,0:T(8,128)(2,1)S(1)}, u32[]{:S(2)}, u32[]{:S(2)}) %collective-permute-start.5) | collective-permute-done | bytes 65568 | tf_op jit(solution)/shard_map/ppermute | solution.py:402
  66.3 0.0 collective-permute-done.4.refs_1_
  66.3 9.2 %near.3.refs_2_ = f32[8,32,128]{2,1,0:T(8,128)S(1)} custom-call(s32[8,27]{1,0:T(8,128)S(1)} %copy-done.4, s32[8]{0:T(128)S(1)} %copy-done.8, bf16[8,32,128]{2,1,0:T(8,128)(2,1)S(1)} %get-tuple-element.20.refs_0_, bf16[8,32,128]{2,1,0:T(8,128)(2,1)S(1)} %collective-permute-done.4.refs_1_, bf16[8,32,128]{2,1,0:T(8,128)(2,1)S(1)} %collective-permute-done.5.refs_2_, ...), custom_call_target="tpu_custom_call" | custom-call | flops 452984832 | bytes 14155776 | tf_op jit(solution)/shard_map/near/pallas_call | solution.py:451
  75.5 0.0 collective-permute-done.3.other
  75.5 2.6 %inner.1 = (f32[16,128]{1,0:T(8,128)S(1)}, f32[16,128]{1,0:T(8,128)S(1)}) custom-call(s32[8,32]{1,0:T(8,128)S(1)} %get-tuple-element.15.far_at, s32[8]{0:T(128)S(1)} %copy-done.6, bf16[16,80,128]{2,1,0:T(8,128)(2,1)S(1)} %all_to_all.16.mine, bf16[16,80,128]{2,1,0:T(8,128)(2,1)S(1)} %collective-permute-done.3.other, ...), custom_call_target="tpu_custom_call" | custom-call | tf_op jit(solution)/shard_map/inner/pallas_call | solution.py:486
  78.2 11.9 %all_to_all.17.sums = f32[32,16,128]{2,1,0:T(8,128)S(1)} all-to-all(f32[32,16,128]{2,1,0:T(8,128)S(1)} %broadcast_in_dim.2), channel_id=1, replica_groups=mesh['contour'=4,'clus'=32] {'clus'}, dimensions={0} | all-to-all | bytes 524288 | tf_op jit(solution)/shard_map/all_to_all | solution.py:504
  90.1 0.0 copy-done.9
  90.1 1.5 %final.1 = (f32[8,2,16,128]{3,2,1,0:T(8,128)}, f32[2,16,16]{2,1,0:T(8,128)}, f32[4,16]{1,0:T(4,128)}) custom-call(f32[2]{0:T(128)S(1)} %copy-done.9, f32[32,16,128]{2,1,0:T(8,128)S(1)} %all_to_all.17.sums, f32[16,128]{1,0:T(8,128)S(1)} %get-tuple-element.24.head, f32[8,32,128]{2,1,0:T(8,128)S(1)} %get-tuple-element.14.refs_1_.refs_4_.refs_3_.base, ...), custom_call_target="tpu_custom_call" | custom-call | tf_op jit(solution)/shard_map/final/pallas_call | solution.py:497
  (10 shorter events, 0.0 us)
Async XLA Ops:
  0.6 0.9 copy-start.1
  1.5 0.9 copy-start.3
  2.4 0.7 copy-start.5
  21.8 22.2 %collective-permute-start.2 = (bf16[16,80,128]{2,1,0:T(8,128)(2,1)S(1)}, bf16[16,80,128]{2,1,0:T(8,128)(2,1)S(1)}, u32[]{:S(2)}, u32[]{:S(2)}) collective-permute-start(bf16[16,80,128]{2,1,0:T(8,128)(2,1)S(1)} %all_to_all.15.mine), channel_id=1, source_target_pairs={{0,1},{1,0},{2,3},{3,2},{4,5},{5,4},{6,7},{7,6},{8,9},{9,8},{10,11... | collective-permute-start | bytes 983048 | tf_op jit(solution)/shard_map/ppermute | solution.py:402
  21.8 22.2 %copy-start.6 = (s32[8]{0:T(128)S(1)}, s32[8]{0:T(128)}, u32[]{:S(2)}) copy-start(s32[8]{0:T(128)} %rows.5) | copy-start | bytes 100
  21.8 22.2 %copy-start = (bf16[8,2,32,128]{3,2,1,0:T(8,128)(2,1)S(1)}, bf16[8,2,32,128]{3,2,1,0:T(8,128)(2,1)}, u32[]{:S(2)}) copy-start(bf16[8,2,32,128]{3,2,1,0:T(8,128)(2,1)} %refs_1_.3) | copy-start | bytes 393220
  21.8 22.2 %copy-start.2 = (bf16[8,2,32,128]{3,2,1,0:T(8,128)(2,1)S(1)}, bf16[8,2,32,128]{3,2,1,0:T(8,128)(2,1)}, u32[]{:S(2)}) copy-start(bf16[8,2,32,128]{3,2,1,0:T(8,128)(2,1)} %refs_2_.1) | copy-start | bytes 393220
  21.8 7.8 %collective-permute-start.1 = (f32[8,32,128]{2,1,0:T(8,128)S(1)}, f32[8,32,128]{2,1,0:T(8,128)S(1)}, u32[]{:S(2)}, u32[]{:S(2)}) collective-permute-start(f32[8,32,128]{2,1,0:T(8,128)S(1)} %get-tuple-element.14.refs_1_.refs_4_.refs_3_.base), channel_id=1, source_target_pairs={{0,31},{1,2},{2,1},{3,4},{4,3},{5,6},{6,5},{7,8},{8,7},{9,10},{10,... | collective-permute-start | bytes 393224 | tf_op jit(solution)/shard_map/ppermute | solution.py:402
  23.2 6.4 %collective-permute-start = (f32[8,32,128]{2,1,0:T(8,128)S(1)}, f32[8,32,128]{2,1,0:T(8,128)S(1)}, u32[]{:S(2)}, u32[]{:S(2)}) collective-permute-start(f32[8,32,128]{2,1,0:T(8,128)S(1)} %get-tuple-element.14.refs_1_.refs_4_.refs_3_.base), channel_id=1, source_target_pairs={{0,1},{1,0},{2,3},{3,2},{4,5},{5,4},{6,7},{7,6},{8,9},{9,8},{10,11... | collective-permute-start | bytes 393224 | tf_op jit(solution)/shard_map/ppermute | solution.py:402
  29.6 0.7 copy-start.4
  30.3 0.7 copy-start.7
  31.0 0.7 copy-start.8
  59.3 16.2 %collective-permute-start.3 = (bf16[16,80,128]{2,1,0:T(8,128)(2,1)S(1)}, bf16[16,80,128]{2,1,0:T(8,128)(2,1)S(1)}, u32[]{:S(2)}, u32[]{:S(2)}) collective-permute-start(bf16[16,80,128]{2,1,0:T(8,128)(2,1)S(1)} %all_to_all.16.mine), channel_id=1, source_target_pairs={{0,1},{1,0},{2,3},{3,2},{4,5},{5,4},{6,7},{7,6},{8,9},{9,8},{10,11... | collective-permute-start | bytes 983048 | tf_op jit(solution)/shard_map/ppermute | solution.py:402
  59.3 30.8 %copy-start.9 = (f32[2]{0:T(128)S(1)}, f32[2]{0:T(128)}, u32[]{:S(2)}) copy-start(f32[2]{0:T(128)} %weight.1) | copy-start | bytes 28
  59.3 7.0 %collective-permute-start.5 = (bf16[8,32,128]{2,1,0:T(8,128)(2,1)S(1)}, bf16[8,32,128]{2,1,0:T(8,128)(2,1)S(1)}, u32[]{:S(2)}, u32[]{:S(2)}) collective-permute-start(bf16[8,32,128]{2,1,0:T(8,128)(2,1)S(1)} %get-tuple-element.20.refs_0_), channel_id=1, source_target_pairs={{0,31},{1,2},{2,1},{3,4},{4,3},{5,6},{6,5},{7,8},{8,7},{9,10},{10,... | collective-permute-start | bytes 196616 | tf_op jit(solution)/shard_map/ppermute | solution.py:402
  60.7 5.6 %collective-permute-start.4 = (bf16[8,32,128]{2,1,0:T(8,128)(2,1)S(1)}, bf16[8,32,128]{2,1,0:T(8,128)(2,1)S(1)}, u32[]{:S(2)}, u32[]{:S(2)}) collective-permute-start(bf16[8,32,128]{2,1,0:T(8,128)(2,1)S(1)} %get-tuple-element.20.refs_0_), channel_id=1, source_target_pairs={{0,1},{1,0},{2,3},{3,2},{4,5},{5,4},{6,7},{7,6},{8,9},{9,8},{10,11... | collective-permute-start | bytes 196616 | tf_op jit(solution)/shard_map/ppermute | solution.py:402

commit v3 on v2

--- a/solution.py
+++ b/solution.py
@@ -16,8 +16,9 @@
 FMAX = 32
 KMAX = 27
 FRONT_MIB = 2
-PIECES = ((0, 1), (1, 2), (3, 2), (5, 3))
-PACK_PIECES = ((0, 4), (4, 2), (6, 2))
+DEPTH = 3
+PIECES = ((0, 2), (2, 2), (4, 2), (6, 2))
+PACK_PIECES = ((0, 4), (4, 4))
 NEAR_MIB = 47
 STAT = 64
 PAY = 80
@@ -157,7 +158,7 @@
         )
         for n, (at, size) in enumerate(PIECES)
     ]
-    for piece in pieces:
+    for piece in pieces[:DEPTH]:
         piece.start()
     me = lax.axis_index("clus")
     flip = (me & 1) * OWN
@@ -168,8 +169,6 @@
             )
             for n, (at, size) in enumerate(PACK_PIECES)
         ]
-        for piece in late:
-            piece.start()
         far = far_list[...]
         owner = far >> 3
         far_at[...] = (((me ^ owner) & 1) * 16 + (owner >> 1)) * OWN + (far & 7)
@@ -188,8 +187,11 @@
                 table[OWN * group + i] = jnp.concatenate([high, low], axis=0)
             else:
                 table[OWN * group + i] = paired(field).astype(BF16)
-    for (at, size), piece in zip(PIECES, pieces):
+    queue = pieces + (late if split else [])
+    for n, ((at, size), piece) in enumerate(zip(PIECES, pieces)):
         piece.wait()
+        if n + DEPTH < len(queue):
+            queue[n + DEPTH].start()
         acc = [jnp.zeros((128, table.shape[1]), F32) for _ in range(size)]
         for k in range(KMAX):
             for j in range(size):
@@ -201,8 +203,10 @@
             out = jnp.transpose(acc[j])
             near[at + j] = out[:32] + out[32:] if split else out
     if split:
-        for (at, size), piece in zip(PACK_PIECES, late):
+        for n, ((at, size), piece) in enumerate(zip(PACK_PIECES, late)):
             piece.wait()
+            if len(pieces) + n + DEPTH < len(queue):
+                queue[len(pieces) + n + DEPTH].start()
             for i in range(at, at + size):
                 pack_one(kept, packed, i)
 
@@ -274,7 +278,7 @@
 
 
 def inner_kernel(far_at, rows, mine, other, *refs):
-    packed, row_basis, near, base, image, keep, sums, head, table, masks = refs
+    packed, row_basis, near, base, image, keep, spread, head, table, masks, sums, out_sems = refs
     far = far_fields(far_at, mine, other, packed, row_basis, table, masks)
     stat = gathered_stat(mine, other)
     hr = column_of(stat, 0, 32, 64)
@@ -337,12 +341,24 @@
         tile = tile + jnp.where(short == k, lane_sum(term), 0.0)
     sums[...] = tile
     head[...] = jnp.where(short == 0, beta, jnp.where(short == 1, hr, jnp.where(short == 2, hi, 0.0)))
-
-
-def final_kernel(weight, sums, head, base, image, solution, moment, arnoldi):
-    tile = sums[0]
-    for slot in range(1, sums.shape[0]):
-        tile = tile + sums[slot]
+    spread_out(sums, spread, out_sems)
+
+
+def prepare_kernel(head, base, image, first, rest):
+    beta, hr, hi = (column_of(head[...], k) for k in range(3))
+    inverse = 1.0 / beta
+    for i in range(OWN):
+        vr, vi = base[i, :PROBES] * inverse, base[i, PROBES:] * inverse
+        first[i, :PROBES] = vr
+        first[i, PROBES:] = vi
+        rest[i, :PROBES] = image[i, :PROBES] - (hr * vr - hi * vi)
+        rest[i, PROBES:] = image[i, PROBES:] - (hr * vi + hi * vr)
+
+
+def final_kernel(weight, mine, other, head, first, rest, solution, moment, arnoldi):
+    tile = mine[0] + other[0]
+    for slot in range(1, mine.shape[0]):
+        tile = tile + (mine[slot] + other[slot])
     top = head[...]
     beta, hr, hi = (column_of(top, k) for k in range(3))
     t2, g12r, g12i, g22, q2r, q2i, g11, q1r, q1i = (column_of(tile, k) for k in range(9))
@@ -357,11 +373,9 @@
     y2i = (g11 * q2i - (g12r * q1i - g12i * q1r)) / det * inv
     wr, wi = weight[0], weight[1]
     factor = 1.0 / (256 * 128)
-    inverse = 1.0 / beta
-    for i in range(OWN):
-        vr, vi = base[i, :PROBES] * inverse, base[i, PROBES:] * inverse
-        tr = image[i, :PROBES] - (hr * vr - hi * vi)
-        ti = image[i, PROBES:] - (hr * vi + hi * vr)
+    for i in range(OWN):
+        vr, vi = first[i, :PROBES], first[i, PROBES:]
+        tr, ti = rest[i, :PROBES], rest[i, PROBES:]
         xr = (y1r * vr - y1i * vi) + (y2r * tr - y2i * ti)
         xi = (y1r * vi + y1i * vr) + (y2r * ti + y2i * tr)
         solution[i, 0] = wr * xr - wi * xi
@@ -483,25 +497,35 @@
 
     (near,) = near_product(False, narrow)
     mine, other = gather_all(spread)
-    sums, head = pl.pallas_call(
+    spread, head = pl.pallas_call(
         inner_kernel,
-        out_shape=(shape((PROBES, 128)), shape((PROBES, 128))),
+        out_shape=(shape((16, PROBES, 128)), shape((PROBES, 128))),
         in_specs=[SMEM, SMEM] + [VMEM] * 8,
-        out_specs=(VMEM, VMEM),
-        scratch_shapes=scratch,
+        out_specs=(ANY, VMEM),
+        scratch_shapes=scratch + [pltpu.VMEM((PROBES, 128), F32), pltpu.SemaphoreType.DMA((16,))],
         compiler_params=params(10),
         name="inner",
     )(far_at, cluster_rows, mine, other, packed, row_basis, near, base, image, keep)
 
-    spread = jnp.broadcast_to(sums[None], (32, PROBES, 128))
+    field = shape((OWN, 32, 128))
+    first, rest = pl.pallas_call(
+        prepare_kernel,
+        out_shape=(field, field),
+        in_specs=[VMEM] * 3,
+        out_specs=(VMEM,) * 2,
+        compiler_params=params(4),
+        cost_estimate=pl.CostEstimate(flops=1 << 20, bytes_accessed=1 << 20, transcendentals=0),
+        name="prepare",
+    )(head, base, image)
+    mine, other = gather_all(spread)
     return pl.pallas_call(
         final_kernel,
         out_shape=(shape((OWN, 2, PROBES, 128)), shape((2, PROBES, PROBES)), shape((4, PROBES))),
-        in_specs=[SMEM] + [VMEM] * 4,
+        in_specs=[SMEM] + [VMEM] * 5,
         out_specs=(VMEM,) * 3,
         compiler_params=params(4),
         name="final",
-    )(weight, lax.all_to_all(spread, "clus", 0, 0), head, base, image)
+    )(weight, mine, other, head, first, rest)
 
 
 def solution(mesh):

time: 93.1 us -> 88 us (0.945)
  Pallas kernels: 30.3 us -> 25.5 us
  blocking collectives: 41.2 us -> 39.8 us
  waiting for transfers between devices: 12 us -> 13.2 us
    all_to_all x1 -> x0, blocking collectives: 11.9 us -> none  [shards(): lax.all_to_all(spread, 'clus', 0, 0)]
    all_to_all x2 -> x3, blocking collectives: 29.3 us -> 39.8 us  [gather_all(): mine = lax.all_to_all(copies, 'clus', 0, 0, axis_index_groups=COLUMNS)]
    pallas_call x2, Pallas kernels: 21.5 us -> 16.3 us  [near_product(): pl.pallas_call(functools.partial(near_kernel, split), out_shape=out_shape...]
    ppermute x6 -> x7, waiting for transfers between devices: 12 us -> 13.2 us  [send(): return lax.ppermute(x, 'clus', pairs)]
    pallas_call x1 -> x2, Pallas kernels: 2.64 us -> 3.15 us  [the longest x1 3.04 us: shards(): pl.pallas_call(inner_kernel, out_shape=(shape((16, PROBES, 128)), shape((...]
    ppermute x6 -> x7, starting transfers between devices: 2.82 us -> 2.82 us  [send(): return lax.ppermute(x, 'clus', pairs)]
  transfers between devices with their start and end apart: 6 -> 7, of which waited for: 2 -> 3; matrix products, arithmetic and copies ran while one was open for 0% -> 0% of each run, Pallas kernels for 23% -> 19%
where the time goes in v3:
time: 88 us; the launch traced here: 86.6 us
  blocking collectives  39.8 us (45%)
  Pallas kernels  25.5 us (29%)
  waiting for transfers between devices  13.2 us (15%)
  local copies, waits for them, and re-layouts  4.5 us (5%)
  starting transfers between devices  2.82 us (3%)
    all_to_all x3, blocking collectives, gather_all(): mine = lax.all_to_all(copies, 'clus', 0, 0, axis_index_groups=COLUMNS)  39.8 us
    pallas_call x2, Pallas kernels, near_product(): pl.pallas_call(functools.partial(near_kernel, split), out_shape=out_shape...  16.3 us
    ppermute x7, waiting for transfers between devices, send(): return lax.ppermute(x, 'clus', pairs)  13.2 us
    unnamed x20, local copies, waits for them, and re-layouts  4.5 us
    pallas_call x1, Pallas kernels, shards(): pl.pallas_call(inner_kernel, out_shape=(shape((16, PROBES, 128)), shape((...  3.04 us
    pallas_call x1, Pallas kernels, shards(): pl.pallas_call(image_kernel, out_shape=(shape((OWN, 32, 128)), shape((OWN...  2.98 us
    ppermute x7, starting transfers between devices, send(): return lax.ppermute(x, 'clus', pairs)  2.82 us
  transfers between devices with their start and end apart: 7, of which 3 were waited for; matrix products, arithmetic and copies ran while one was open for 0% of the time, Pallas kernels for 19%

profile of v3, /device:TPU:0, one launch (start us, length us, event | category | flops | bytes accessed | tf_op | source)
XLA Modules:
  0.0 86.6 jit_solution(8110635275536759335)
XLA Ops:
  0.6 0.0 copy-start.1
  0.6 0.9 %copy-done.1 = bf16[8,2,32,128]{3,2,1,0:T(8,128)(2,1)S(1)} copy-done((bf16[8,2,32,128]{3,2,1,0:T(8,128)(2,1)S(1)}, bf16[8,2,32,128]{3,2,1,0:T(8,128)(2,1)}, u32[]{:S(2)}) %copy-start.1) | copy-done | bytes 131096
  1.5 0.9 %copy-done.3 = f32[8,2,16,128]{3,2,1,0:T(8,128)S(1)} copy-done((f32[8,2,16,128]{3,2,1,0:T(8,128)S(1)}, f32[8,2,16,128]{3,2,1,0:T(8,128)}, u32[]{:S(2)}) %copy-start.3) | copy-done | bytes 131096
  2.4 0.7 copy-done.5
  3.1 1.6 %front.1 = (f32[8,32,128]{2,1,0:T(8,128)S(1)}, bf16[16,80,128]{2,1,0:T(8,128)(2,1)S(1)}) custom-call(s32[8]{0:T(128)S(1)} %copy-done.5, f32[8,2,16,128]{3,2,1,0:T(8,128)S(1)} %copy-done.3, bf16[8,2,32,128]{3,2,1,0:T(8,128)(2,1)S(1)} %copy-done.1), custom_call_target="tpu_custom_call" | custom-call | tf_op jit(solution)/shard_map/front/pallas_call | solution.py:436
  4.7 17.1 %all_to_all.15.mine = bf16[16,80,128]{2,1,0:T(8,128)(2,1)S(1)} all-to-all(bf16[16,80,128]{2,1,0:T(8,128)(2,1)S(1)} %get-tuple-element.18), channel_id=1, replica_groups={{0,2,4,6,8,10,12,14,16,18,20,22,24,26,28,30},{1,3,5,7,9,11,13,15,17,19,..., dimensions={0} | all-to-all | bytes 655360 | tf_op jit(solution)/shard_map/all_to_all | solution.py:420
  21.8 0.0 collective-permute-start.2
  21.8 1.4 %collective-permute-start.1 = (f32[8,32,128]{2,1,0:T(8,128)S(1)}, f32[8,32,128]{2,1,0:T(8,128)S(1)}, u32[]{:S(2)}, u32[]{:S(2)}) collective-permute-start(f32[8,32,128]{2,1,0:T(8,128)S(1)} %get-tuple-element.16.refs_1_.refs_4_.refs_3_.base), channel_id=1, source_target_pairs={{0,31},{1,2},{2,1},{3,4},{4,3},{5,6},{6,5},{7,8},{8,7},{9,10},{10,... | collective-permute-start | bytes 393224 | tf_op jit(solution)/shard_map/ppermute | solution.py:416
  23.2 0.0 collective-permute-start
  23.2 6.4 %collective-permute-done.1.refs_3_ = f32[8,32,128]{2,1,0:T(8,128)S(1)} collective-permute-done((f32[8,32,128]{2,1,0:T(8,128)S(1)}, f32[8,32,128]{2,1,0:T(8,128)S(1)}, u32[]{:S(2)}, u32[]{:S(2)}) %collective-permute-start.1) | collective-permute-done | bytes 131104 | tf_op jit(solution)/shard_map/ppermute | solution.py:416
  29.6 0.0 collective-permute-done.refs_2_
  29.6 0.7 copy-done.4
  30.3 0.7 copy-done.7
  31.0 0.7 copy-done.8
  31.7 9.3 %near.2 = (f32[8,32,128]{2,1,0:T(8,128)S(1)}, bf16[8,128,1024]{2,1,0:T(8,128)(2,1)S(1)}, s32[8,32]{1,0:T(8,128)S(1)}) custom-call(s32[8,27]{1,0:T(8,128)S(1)} %copy-done.4, s32[8]{0:T(128)S(1)} %copy-done.8, s32[8,32]{1,0:T(8,128)S(1)} %copy-done.7, f32[8,32,128]{2,1,0:T(8,128)S(1)} %get-tuple-element.16.refs_1_.refs_4_.refs_3_.base, ...), custom_call_target="tpu_custom_call" | custom-call | flops 452984832 | bytes 14155776 | tf_op jit(solution)/shard_map/near/pallas_call | solution.py:465
  40.9 0.0 collective-permute-done.2.other
  41.0 3.0 %image.1 = (f32[8,32,128]{2,1,0:T(8,128)S(1)}, bf16[8,32,128]{2,1,0:T(8,128)(2,1)S(1)}, bf16[16,80,128]{2,1,0:T(8,128)(2,1)S(1)}, f32[16,128]{1,0:T(8,128)S(1)}) custom-call(s32[8,32]{1,0:T(8,128)S(1)} %get-tuple-element.17.far_at, s32[8]{0:T(128)S(1)} %copy-done.6, bf16[16,80,128]{2,1,0:T(8,128)(2,1)S(1)} %all_to_all.15.mine, ...), custom_call_target="tpu_custom_call" | custom-call | tf_op jit(solution)/shard_map/image/pallas_call | solution.py:483
  44.0 12.2 %all_to_all.16.mine = bf16[16,80,128]{2,1,0:T(8,128)(2,1)S(1)} all-to-all(bf16[16,80,128]{2,1,0:T(8,128)(2,1)S(1)} %get-tuple-element.21), channel_id=1, replica_groups={{0,2,4,6,8,10,12,14,16,18,20,22,24,26,28,30},{1,3,5,7,9,11,13,15,17,19,..., dimensions={0} | all-to-all | bytes 655360 | tf_op jit(solution)/shard_map/all_to_all | solution.py:420
  56.2 0.0 collective-permute-start.3
  56.2 1.4 %collective-permute-start.5 = (bf16[8,32,128]{2,1,0:T(8,128)(2,1)S(1)}, bf16[8,32,128]{2,1,0:T(8,128)(2,1)S(1)}, u32[]{:S(2)}, u32[]{:S(2)}) collective-permute-start(bf16[8,32,128]{2,1,0:T(8,128)(2,1)S(1)} %get-tuple-element.22.refs_0_), channel_id=1, source_target_pairs={{0,31},{1,2},{2,1},{3,4},{4,3},{5,6},{6,5},{7,8},{8,7},{9,10},{10,... | collective-permute-start | bytes 196616 | tf_op jit(solution)/shard_map/ppermute | solution.py:416
  57.6 0.0 collective-permute-start.4
  57.6 5.6 %collective-permute-done.5.refs_2_ = bf16[8,32,128]{2,1,0:T(8,128)(2,1)S(1)} collective-permute-done((bf16[8,32,128]{2,1,0:T(8,128)(2,1)S(1)}, bf16[8,32,128]{2,1,0:T(8,128)(2,1)S(1)}, u32[]{:S(2)}, u32[]{:S(2)}) %collective-permute-start.5) | collective-permute-done | bytes 65568 | tf_op jit(solution)/shard_map/ppermute | solution.py:416
  63.2 0.0 collective-permute-done.4.refs_1_
  63.2 7.0 %near.3.refs_2_ = f32[8,32,128]{2,1,0:T(8,128)S(1)} custom-call(s32[8,27]{1,0:T(8,128)S(1)} %copy-done.4, s32[8]{0:T(128)S(1)} %copy-done.8, bf16[8,32,128]{2,1,0:T(8,128)(2,1)S(1)} %get-tuple-element.22.refs_0_, bf16[8,32,128]{2,1,0:T(8,128)(2,1)S(1)} %collective-permute-done.4.refs_1_, bf16[8,32,128]{2,1,0:T(8,128)(2,1)S(1)} %collective-permute-done.5.refs_2_, ...), custom_call_target="tpu_custom_call" | custom-call | flops 452984832 | bytes 14155776 | tf_op jit(solution)/shard_map/near/pallas_call | solution.py:465
  70.3 0.0 collective-permute-done.3.other
  70.3 3.0 %inner.1 = (f32[16,16,128]{2,1,0:T(8,128)S(1)}, f32[16,128]{1,0:T(8,128)S(1)}) custom-call(s32[8,32]{1,0:T(8,128)S(1)} %get-tuple-element.17.far_at, s32[8]{0:T(128)S(1)} %copy-done.6, bf16[16,80,128]{2,1,0:T(8,128)(2,1)S(1)} %all_to_all.16.mine, bf16[16,80,128]{2,1,0:T(8,128)(2,1)S(1)} %collective-permute-done.3.other, ...), custom_call_target="tpu_custom_call" | custom-call | tf_op jit(solution)/shard_map/inner/pallas_call | solution.py:500
  73.3 10.4 %all_to_all.17.mine = f32[16,16,128]{2,1,0:T(8,128)S(1)} all-to-all(f32[16,16,128]{2,1,0:T(8,128)S(1)} %get-tuple-element.25), channel_id=1, replica_groups={{0,2,4,6,8,10,12,14,16,18,20,22,24,26,28,30},{1,3,5,7,9,11,13,15,17,19,..., dimensions={0} | all-to-all | bytes 262144 | tf_op jit(solution)/shard_map/all_to_all | solution.py:420
  83.8 0.0 collective-permute-start.6
  83.8 0.1 prepare.1
  83.9 1.2 %collective-permute-done.6.other = f32[16,16,128]{2,1,0:T(8,128)S(1)} collective-permute-done((f32[16,16,128]{2,1,0:T(8,128)S(1)}, f32[16,16,128]{2,1,0:T(8,128)S(1)}, u32[]{:S(2)}, u32[]{:S(2)}) %collective-permute-start.6) | collective-permute-done | bytes 131104 | tf_op jit(solution)/shard_map/ppermute | solution.py:416
  85.1 0.0 copy-done.9
  85.1 1.5 %final.1 = (f32[8,2,16,128]{3,2,1,0:T(8,128)}, f32[2,16,16]{2,1,0:T(8,128)}, f32[4,16]{1,0:T(4,128)}) custom-call(f32[2]{0:T(128)S(1)} %copy-done.9, f32[16,16,128]{2,1,0:T(8,128)S(1)} %all_to_all.17.mine, f32[16,16,128]{2,1,0:T(8,128)S(1)} %collective-permute-done.6.other, f32[16,128]{1,0:T(8,128)S(1)} %get-tuple-element.26.head, ...), custom_call_target="tpu_custom_call" | custom-call | tf_op jit(solution)/shard_map/final/pallas_call | solution.py:521
  (12 shorter events, 0.0 us)
Async XLA Ops:
  0.6 0.9 %copy-start.1 = (bf16[8,2,32,128]{3,2,1,0:T(8,128)(2,1)S(1)}, bf16[8,2,32,128]{3,2,1,0:T(8,128)(2,1)}, u32[]{:S(2)}) copy-start(bf16[8,2,32,128]{3,2,1,0:T(8,128)(2,1)} %refs_2_.1) | copy-start | bytes 393220
  1.5 0.9 %copy-start.3 = (f32[8,2,16,128]{3,2,1,0:T(8,128)S(1)}, f32[8,2,16,128]{3,2,1,0:T(8,128)}, u32[]{:S(2)}) copy-start(f32[8,2,16,128]{3,2,1,0:T(8,128)} %probes.1) | copy-start | bytes 393220
  2.4 0.7 copy-start.5
  21.8 19.1 %collective-permute-start.2 = (bf16[16,80,128]{2,1,0:T(8,128)(2,1)S(1)}, bf16[16,80,128]{2,1,0:T(8,128)(2,1)S(1)}, u32[]{:S(2)}, u32[]{:S(2)}) collective-permute-start(bf16[16,80,128]{2,1,0:T(8,128)(2,1)S(1)} %all_to_all.15.mine), channel_id=1, source_target_pairs={{0,1},{1,0},{2,3},{3,2},{4,5},{5,4},{6,7},{7,6},{8,9},{9,8},{10,11... | collective-permute-start | bytes 983048 | tf_op jit(solution)/shard_map/ppermute | solution.py:416
  21.8 19.1 %copy-start.6 = (s32[8]{0:T(128)S(1)}, s32[8]{0:T(128)}, u32[]{:S(2)}) copy-start(s32[8]{0:T(128)} %rows.5) | copy-start | bytes 100
  21.8 19.1 %copy-start = (bf16[8,2,32,128]{3,2,1,0:T(8,128)(2,1)S(1)}, bf16[8,2,32,128]{3,2,1,0:T(8,128)(2,1)}, u32[]{:S(2)}) copy-start(bf16[8,2,32,128]{3,2,1,0:T(8,128)(2,1)} %refs_1_.3) | copy-start | bytes 393220
  21.8 19.1 %copy-start.2 = (bf16[8,2,32,128]{3,2,1,0:T(8,128)(2,1)S(1)}, bf16[8,2,32,128]{3,2,1,0:T(8,128)(2,1)}, u32[]{:S(2)}) copy-start(bf16[8,2,32,128]{3,2,1,0:T(8,128)(2,1)} %refs_2_.1) | copy-start | bytes 393220
  21.8 7.8 %collective-permute-start.1 = (f32[8,32,128]{2,1,0:T(8,128)S(1)}, f32[8,32,128]{2,1,0:T(8,128)S(1)}, u32[]{:S(2)}, u32[]{:S(2)}) collective-permute-start(f32[8,32,128]{2,1,0:T(8,128)S(1)} %get-tuple-element.16.refs_1_.refs_4_.refs_3_.base), channel_id=1, source_target_pairs={{0,31},{1,2},{2,1},{3,4},{4,3},{5,6},{6,5},{7,8},{8,7},{9,10},{10,... | collective-permute-start | bytes 393224 | tf_op jit(solution)/shard_map/ppermute | solution.py:416
  23.2 6.4 %collective-permute-start = (f32[8,32,128]{2,1,0:T(8,128)S(1)}, f32[8,32,128]{2,1,0:T(8,128)S(1)}, u32[]{:S(2)}, u32[]{:S(2)}) collective-permute-start(f32[8,32,128]{2,1,0:T(8,128)S(1)} %get-tuple-element.16.refs_1_.refs_4_.refs_3_.base), channel_id=1, source_target_pairs={{0,1},{1,0},{2,3},{3,2},{4,5},{5,4},{6,7},{7,6},{8,9},{9,8},{10,11... | collective-permute-start | bytes 393224 | tf_op jit(solution)/shard_map/ppermute | solution.py:416
  29.6 0.7 copy-start.4
  30.3 0.7 copy-start.7
  31.0 0.7 copy-start.8
  56.2 14.1 %collective-permute-start.3 = (bf16[16,80,128]{2,1,0:T(8,128)(2,1)S(1)}, bf16[16,80,128]{2,1,0:T(8,128)(2,1)S(1)}, u32[]{:S(2)}, u32[]{:S(2)}) collective-permute-start(bf16[16,80,128]{2,1,0:T(8,128)(2,1)S(1)} %all_to_all.16.mine), channel_id=1, source_target_pairs={{0,1},{1,0},{2,3},{3,2},{4,5},{5,4},{6,7},{7,6},{8,9},{9,8},{10,11... | collective-permute-start | bytes 983048 | tf_op jit(solution)/shard_map/ppermute | solution.py:416
  56.2 28.9 %copy-start.9 = (f32[2]{0:T(128)S(1)}, f32[2]{0:T(128)}, u32[]{:S(2)}) copy-start(f32[2]{0:T(128)} %weight.1) | copy-start | bytes 28
  56.2 7.0 %collective-permute-start.5 = (bf16[8,32,128]{2,1,0:T(8,128)(2,1)S(1)}, bf16[8,32,128]{2,1,0:T(8,128)(2,1)S(1)}, u32[]{:S(2)}, u32[]{:S(2)}) collective-permute-start(bf16[8,32,128]{2,1,0:T(8,128)(2,1)S(1)} %get-tuple-element.22.refs_0_), channel_id=1, source_target_pairs={{0,31},{1,2},{2,1},{3,4},{4,3},{5,6},{6,5},{7,8},{8,7},{9,10},{10,... | collective-permute-start | bytes 196616 | tf_op jit(solution)/shard_map/ppermute | solution.py:416
  57.6 5.6 %collective-permute-start.4 = (bf16[8,32,128]{2,1,0:T(8,128)(2,1)S(1)}, bf16[8,32,128]{2,1,0:T(8,128)(2,1)S(1)}, u32[]{:S(2)}, u32[]{:S(2)}) collective-permute-start(bf16[8,32,128]{2,1,0:T(8,128)(2,1)S(1)} %get-tuple-element.22.refs_0_), channel_id=1, source_target_pairs={{0,1},{1,0},{2,3},{3,2},{4,5},{5,4},{6,7},{7,6},{8,9},{9,8},{10,11... | collective-permute-start | bytes 196616 | tf_op jit(solution)/shard_map/ppermute | solution.py:416
  83.8 1.3 %collective-permute-start.6 = (f32[16,16,128]{2,1,0:T(8,128)S(1)}, f32[16,16,128]{2,1,0:T(8,128)S(1)}, u32[]{:S(2)}, u32[]{:S(2)}) collective-permute-start(f32[16,16,128]{2,1,0:T(8,128)S(1)} %all_to_all.17.mine), channel_id=1, source_target_pairs={{0,1},{1,0},{2,3},{3,2},{4,5},{5,4},{6,7},{7,6},{8,9},{9,8},{10,11... | collective-permute-start | bytes 393224 | tf_op jit(solution)/shard_map/ppermute | solution.py:416

commit v4 on v3

--- a/solution.py
+++ b/solution.py
@@ -25,7 +25,6 @@
 VMEM = pl.BlockSpec(memory_space=pltpu.VMEM)
 SMEM = pl.BlockSpec(memory_space=pltpu.SMEM)
 HBM = pl.BlockSpec(memory_space=pltpu.HBM)
-ANY = pl.BlockSpec(memory_space=pl.ANY)
 
 
 def dot_nt(left, right):
@@ -91,11 +90,11 @@
     return jnp.sum(jnp.where(keep, tile, 0.0), axis=1, keepdims=True)
 
 
-def gathered_stat(mine, other):
+def gathered_stat(*parts):
     total = jnp.zeros((PROBES, 128), F32)
-    for ref in (mine, other):
-        for slot in range(16):
-            total = total + ref[slot, STAT:PAY].astype(F32)
+    for part in parts:
+        for slot in range(part.shape[0]):
+            total = total + part[slot, STAT:PAY].astype(F32)
     return total
 
 
@@ -117,14 +116,11 @@
         copy.wait()
 
 
-def front_kernel(rows, probes, col_basis, base, spread, pay, out_sems):
-    lane = lanes(2 * PROBES)
+def front_kernel(base, col_basis, spread, pay, out_sems):
     acc = jnp.zeros((PROBES, 128), F32)
     fields = []
     for i in range(OWN):
-        raw = jnp.concatenate([probes[i, 0], probes[i, 1]], axis=0)
-        field = jnp.where(lane < rows[i], raw, 0.0)
-        base[i] = field
+        field = base[i]
         fields.append(field)
         square = field * field
         acc = acc + square[:PROBES] + square[PROBES:]
@@ -146,10 +142,10 @@
         packed[i, :, 128 * g : 128 * g + 128] = jnp.concatenate([high, low], axis=0)
 
 
-def near_kernel(split, near_list, near_count, *refs):
+def near_kernel(split, meta, *refs):
     if split:
-        far_list, own, partner, other, blocks, coupling, near, packed, far_at = refs[:9]
-        table, held, sems, kept, more = refs[9:]
+        own, partner, other, blocks, coupling, near, packed = refs[:7]
+        table, held, sems, kept, more = refs[7:]
     else:
         own, partner, other, blocks, near, table, held, sems = refs
     pieces = [
@@ -169,12 +165,9 @@
             )
             for n, (at, size) in enumerate(PACK_PIECES)
         ]
-        far = far_list[...]
-        owner = far >> 3
-        far_at[...] = (((me ^ owner) & 1) * 16 + (owner >> 1)) * OWN + (far & 7)
 
     def place(i, k):
-        local = near_list[i, k] - me * OWN
+        local = meta[i, k] - me * OWN
         return jnp.where(
             local < 0, local + 3 * OWN - flip, jnp.where(local < OWN, local, local + flip)
         )
@@ -196,7 +189,7 @@
         for k in range(KMAX):
             for j in range(size):
                 vec = table[place(at + j, k)]
-                vec = jnp.where(k < near_count[at + j], vec, jnp.zeros_like(vec))
+                vec = jnp.where(k < meta[OWN, at + j], vec, jnp.zeros_like(vec))
                 mat = jnp.concatenate([held[at + j, k, 0], held[at + j, k, 1]], axis=1)
                 acc[j] = acc[j] + dot_nt(mat, vec)
         for j in range(size):
@@ -211,11 +204,12 @@
                 pack_one(kept, packed, i)
 
 
-def far_fields(far_at, mine, other, packed, row_basis, table, masks):
-    for half, ref in enumerate((mine, other)):
-        for slot in range(16):
-            at = 2 * (16 * half + slot)
-            table[at : at + 2] = ref[slot, 0:STAT].reshape(2, RANK, 128)
+def far_fields(far_list, parts, packed, row_basis, table, masks):
+    parity = lax.axis_index("clus") & 1
+    for half, part in enumerate(parts):
+        for slot in range(part.shape[0]):
+            owner = slot if len(parts) == 1 else 2 * slot + (parity ^ half)
+            table[pl.ds(2 * owner, 2)] = part[slot, 0:STAT].reshape(2, RANK, 128)
     block = lanes(RANK) // RANK
     for b in range(4):
         masks[b] = jnp.where(block == b, 1.0, 0.0).astype(BF16)
@@ -223,7 +217,7 @@
     for i in range(OWN):
         rows = []
         for f in range(FMAX):
-            at = far_at[i, f]
+            at = far_list[i, f]
             rows.append(table[at >> 2] * masks[at & 3])
         acc = dot_nn(packed[i], jnp.concatenate(rows, axis=0))
         folded.append(acc[:64] + acc[64:])
@@ -248,15 +242,16 @@
     return [x[0:32] + x[32:64] for x in out]
 
 
-def image_kernel(far_at, rows, mine, other, *refs):
-    packed, row_basis, col_basis, near, base, image, narrow, spread, keep = refs[:-4]
+def image_kernel(far_list, rows, whole, *refs):
+    packed, row_basis, col_basis, near, base, image, narrow, spread = refs[:-4]
     table, masks, pay, out_sems = refs[-4:]
-    far = far_fields(far_at, mine, other, packed, row_basis, table, masks)
-    beta = jnp.sqrt(column_of(gathered_stat(mine, other), 0, 32, 64) + 1e-06)
+    far = far_fields(far_list, (whole,), packed, row_basis, table, masks)
+    beta = jnp.sqrt(column_of(gathered_stat(whole), 0, 32, 64) + 1e-06)
     inverse = twice(1.0 / beta)
     lane = lanes(2 * PROBES)
     acc_re = jnp.zeros((PROBES, 128), F32)
     acc_im = jnp.zeros((PROBES, 128), F32)
+    acc_sq = jnp.zeros((PROBES, 128), F32)
     values = []
     for i in range(OWN):
         value = jnp.where(lane < rows[i], near[i] + far[i], 0.0) * inverse
@@ -270,20 +265,22 @@
         wr, wi = values[i][:PROBES], values[i][PROBES:]
         acc_re = acc_re + vr * wr + vi * wi
         acc_im = acc_im + vr * wi - vi * wr
+        square = base[i] * base[i]
+        acc_sq = acc_sq + square[:PROBES] + square[PROBES:]
     pay[0:32] = side_by_side(wide[:4]).astype(BF16)
     pay[32:64] = side_by_side(wide[4:]).astype(BF16)
-    pay[STAT:PAY] = (three_way(lane_sum(acc_re), 0) + three_way(lane_sum(acc_im), 1)).astype(BF16)
-    keep[...] = jnp.broadcast_to(beta, (PROBES, 128))
+    stats = (acc_re, acc_im, acc_sq)
+    pay[STAT:PAY] = sum(three_way(lane_sum(x), n) for n, x in enumerate(stats)).astype(BF16)
     spread_out(pay, spread, out_sems)
 
 
-def inner_kernel(far_at, rows, mine, other, *refs):
-    packed, row_basis, near, base, image, keep, spread, head, table, masks, sums, out_sems = refs
-    far = far_fields(far_at, mine, other, packed, row_basis, table, masks)
+def inner_kernel(far_list, rows, mine, other, *refs):
+    packed, row_basis, near, base, image, spread, head, table, masks, sums, out_sems = refs
+    far = far_fields(far_list, (mine, other), packed, row_basis, table, masks)
     stat = gathered_stat(mine, other)
     hr = column_of(stat, 0, 32, 64)
     hi = column_of(stat, 1, 33, 65)
-    beta = column_of(keep[...], 0)
+    beta = jnp.sqrt(column_of(stat, 2, 34, 66) + 1e-06)
     inverse = twice(1.0 / beta)
     lane = lanes(2 * PROBES)
 
@@ -355,10 +352,10 @@
         rest[i, PROBES:] = image[i, PROBES:] - (hr * vi + hi * vr)
 
 
-def final_kernel(weight, mine, other, head, first, rest, solution, moment, arnoldi):
-    tile = mine[0] + other[0]
-    for slot in range(1, mine.shape[0]):
-        tile = tile + (mine[slot] + other[slot])
+def final_kernel(weight, whole, head, first, rest, solution, moment, arnoldi):
+    tile = whole[0]
+    for slot in range(1, 32):
+        tile = tile + whole[slot]
     top = head[...]
     beta, hr, hi = (column_of(top, k) for k in range(3))
     t2, g12r, g12i, g22, q2r, q2i, g11, q1r, q1i = (column_of(tile, k) for k in range(9))
@@ -408,8 +405,8 @@
 
 
 CORE = [(i, i ^ 1) for i in range(32)]
+COLUMNS = [list(range(k, 32, 2)) for k in range(2)]
 SIDE = [(i, (i + 1 if i % 2 else i - 1) % 32) for i in range(32)]
-COLUMNS = [list(range(k, 32, 2)) for k in range(2)]
 
 
 def send(x, pairs):
@@ -417,6 +414,10 @@
 
 
 def gather_all(copies):
+    return lax.all_to_all(copies, "clus", 0, 0)
+
+
+def gather_halves(copies):
     mine = lax.all_to_all(copies, "clus", 0, 0, axis_index_groups=COLUMNS)
     return mine, send(mine, CORE)
 
@@ -433,15 +434,24 @@
     far_coupling,
     weight,
 ):
-    base, spread = pl.pallas_call(
-        front_kernel,
-        out_shape=(shape((OWN, 32, 128)), shape((16, PAY, 128), BF16)),
-        in_specs=[SMEM, VMEM, VMEM],
-        out_specs=(VMEM, ANY),
-        scratch_shapes=[pltpu.VMEM((PAY, 128), BF16), pltpu.SemaphoreType.DMA((16,))],
-        compiler_params=params(FRONT_MIB),
-        name="front",
-    )(cluster_rows, probes, col_basis)
+    rows_iota = lax.broadcasted_iota(jnp.int32, (OWN, 1, 1, 128), 3)
+    live = rows_iota < cluster_rows[:, None, None, None]
+    base = jnp.where(live, probes, 0.0).reshape(OWN, 32, 128)
+    meta = jnp.pad(near_list, ((0, 1), (0, 0))) + jnp.pad(
+        near_count[None], ((OWN, 0), (0, KMAX - OWN))
+    )
+
+    def front():
+        return pl.pallas_call(
+            front_kernel,
+            out_shape=shape((32, PAY, 128), BF16),
+            in_specs=[VMEM, VMEM],
+            out_specs=HBM,
+            scratch_shapes=[pltpu.VMEM((PAY, 128), BF16), pltpu.SemaphoreType.DMA((32,))],
+            compiler_params=params(FRONT_MIB),
+            cost_estimate=pl.CostEstimate(flops=1 << 20, bytes_accessed=1 << 20, transcendentals=0),
+            name="front",
+        )(base, col_basis)
 
     def near_product(split, field):
         partner = send(field, CORE)
@@ -455,17 +465,17 @@
         arguments = [field, partner, other, near_blocks]
         in_specs = [VMEM, VMEM, VMEM, HBM]
         if split:
-            out_shape += [shape((OWN, 128, 1024), BF16), shape((OWN, FMAX), jnp.int32)]
+            out_shape += [shape((OWN, 128, 1024), BF16)]
             scratch += [
                 pltpu.VMEM((OWN, FMAX, 2, RANK, RANK), F32),
                 pltpu.SemaphoreType.DMA((len(PACK_PIECES),)),
             ]
-            arguments = [far_list] + arguments + [far_coupling]
-            in_specs = [VMEM] + in_specs + [HBM]
+            arguments += [far_coupling]
+            in_specs += [HBM]
         return pl.pallas_call(
             functools.partial(near_kernel, split),
             out_shape=out_shape,
-            in_specs=[SMEM, SMEM] + in_specs,
+            in_specs=[SMEM] + in_specs,
             out_specs=[VMEM] * len(out_shape),
             scratch_shapes=scratch,
             compiler_params=params(NEAR_MIB),
@@ -475,37 +485,37 @@
                 transcendentals=0,
             ),
             name="near",
-        )(near_list, near_count, *arguments)
-
-    near, packed, far_at = near_product(True, base)
-    mine, other = gather_all(spread)
+        )(meta, *arguments)
+
+    spread = front()
+    near, packed = near_product(True, base)
+    whole = gather_all(spread)
     scratch = [pltpu.VMEM((64, RANK, 128), BF16), pltpu.VMEM((4, RANK, 128), BF16)]
-    image, narrow, spread, keep = pl.pallas_call(
+    image, narrow, spread = pl.pallas_call(
         image_kernel,
         out_shape=(
             shape((OWN, 32, 128)),
             shape((OWN, 32, 128), BF16),
             shape((16, PAY, 128), BF16),
-            shape((PROBES, 128)),
         ),
-        in_specs=[SMEM, SMEM] + [VMEM] * 7,
-        out_specs=(VMEM, VMEM, ANY, VMEM),
+        in_specs=[SMEM, SMEM] + [VMEM] * 6,
+        out_specs=(VMEM, VMEM, HBM),
         scratch_shapes=scratch + [pltpu.VMEM((PAY, 128), BF16), pltpu.SemaphoreType.DMA((16,))],
         compiler_params=params(10),
         name="image",
-    )(far_at, cluster_rows, mine, other, packed, row_basis, col_basis, near, base)
+    )(far_list, cluster_rows, whole, packed, row_basis, col_basis, near, base)
 
     (near,) = near_product(False, narrow)
-    mine, other = gather_all(spread)
+    mine, other = gather_halves(spread)
     spread, head = pl.pallas_call(
         inner_kernel,
-        out_shape=(shape((16, PROBES, 128)), shape((PROBES, 128))),
-        in_specs=[SMEM, SMEM] + [VMEM] * 8,
-        out_specs=(ANY, VMEM),
-        scratch_shapes=scratch + [pltpu.VMEM((PROBES, 128), F32), pltpu.SemaphoreType.DMA((16,))],
+        out_shape=(shape((32, PROBES, 128)), shape((PROBES, 128))),
+        in_specs=[SMEM, SMEM] + [VMEM] * 7,
+        out_specs=(HBM, VMEM),
+        scratch_shapes=scratch + [pltpu.VMEM((PROBES, 128), F32), pltpu.SemaphoreType.DMA((32,))],
         compiler_params=params(10),
         name="inner",
-    )(far_at, cluster_rows, mine, other, packed, row_basis, near, base, image, keep)
+    )(far_list, cluster_rows, mine, other, packed, row_basis, near, base, image)
 
     field = shape((OWN, 32, 128))
     first, rest = pl.pallas_call(
@@ -517,15 +527,15 @@
         cost_estimate=pl.CostEstimate(flops=1 << 20, bytes_accessed=1 << 20, transcendentals=0),
         name="prepare",
     )(head, base, image)
-    mine, other = gather_all(spread)
+    whole = gather_all(spread)
     return pl.pallas_call(
         final_kernel,
         out_shape=(shape((OWN, 2, PROBES, 128)), shape((2, PROBES, PROBES)), shape((4, PROBES))),
-        in_specs=[SMEM] + [VMEM] * 5,
+        in_specs=[SMEM] + [VMEM] * 4,
         out_specs=(VMEM,) * 3,
         compiler_params=params(4),
         name="final",
-    )(weight, mine, other, head, first, rest)
+    )(weight, whole, head, first, rest)
 
 
 def solution(mesh):

time: 88 us -> 86 us (0.977)
  blocking collectives: 39.8 us -> 12 us
  starting transfers between devices: 2.82 us -> 18.8 us
  waiting for transfers between devices: 13.2 us -> 23.4 us
  local copies, waits for them, and re-layouts: 4.5 us -> 0.92 us
  other arithmetic: 0 us -> 2.35 us
    all_to_all x3 -> x1, blocking collectives: 39.8 us -> 12 us  [gather_halves(): mine = lax.all_to_all(copies, 'clus', 0, 0, axis_index_groups=COLUMNS)]
    all_to_all x0 -> x2, starting transfers between devices: none -> 12.3 us  [gather_all(): return lax.all_to_all(copies, 'clus', 0, 0)]
    all_to_all x0 -> x2, waiting for transfers between devices: none -> 8.8 us  [gather_all(): return lax.all_to_all(copies, 'clus', 0, 0)]
    ppermute x7 -> x5, starting transfers between devices: 2.82 us -> 6.42 us  [send(): return lax.ppermute(x, 'clus', pairs)]
    unnamed x20 -> x12, local copies, waits for them, and re-layouts: 4.5 us -> 0.92 us
    ppermute x7 -> x5, waiting for transfers between devices: 13.2 us -> 14.6 us  [send(): return lax.ppermute(x, 'clus', pairs)]
    select_n x0 -> x1, other arithmetic: none -> 0.92 us  [shards(): base = jnp.where(live, probes, 0.0).reshape(OWN, 32, 128)]
  transfers between devices with their start and end apart: 7 -> 7, of which waited for: 3 -> 3; matrix products, arithmetic and copies ran while one was open for 0% -> 1% of each run, Pallas kernels for 19% -> 20%
where the time goes in v4:
time: 86 us; the launch traced here: 84.4 us
  Pallas kernels  26.2 us (30%)
  waiting for transfers between devices  23.4 us (27%)
  starting transfers between devices  18.8 us (22%)
  blocking collectives  12 us (14%)
  other arithmetic  2.35 us (3%)
  local copies, waits for them, and re-layouts  0.92 us (1%)
    pallas_call x2, Pallas kernels, near_product(): pl.pallas_call(functools.partial(near_kernel, split), out_shape=out_shape...  16.4 us
    ppermute x5, waiting for transfers between devices, send(): return lax.ppermute(x, 'clus', pairs)  14.6 us
    all_to_all x2, starting transfers between devices, gather_all(): return lax.all_to_all(copies, 'clus', 0, 0)  12.3 us
    all_to_all x1, blocking collectives, gather_halves(): mine = lax.all_to_all(copies, 'clus', 0, 0, axis_index_groups=COLUMNS)  12 us
    all_to_all x2, waiting for transfers between devices, gather_all(): return lax.all_to_all(copies, 'clus', 0, 0)  8.8 us
    ppermute x5, starting transfers between devices, send(): return lax.ppermute(x, 'clus', pairs)  6.42 us
    pallas_call x1, Pallas kernels, shards(): pl.pallas_call(inner_kernel, out_shape=(shape((32, PROBES, 128)), shape((...  3.62 us
    pallas_call x1, Pallas kernels, shards(): pl.pallas_call(image_kernel, out_shape=(shape((OWN, 32, 128)), shape((OWN...  2.95 us
  transfers between devices with their start and end apart: 7, of which 3 were waited for; matrix products, arithmetic and copies ran while one was open for 1% of the time, Pallas kernels for 20%

profile of v4, /device:TPU:0, one launch (start us, length us, event | category | flops | bytes accessed | tf_op | source)
XLA Modules:
  0.0 84.4 jit_solution(2810496690747599554)
XLA Ops:
  0.6 0.7 iota_compare_fusion
  1.4 0.9 %broadcast_select_fusion = f32[8,2,16,128]{3,2,1,0:T(8,128)S(1)} fusion(f32[8,2,16,128]{3,2,1,0:T(8,128)} %param.10, pred[8,128]{1,0:T(8,128)(4,1)S(1)} %iota_compare_fusion), kind=kLoop, calls=%fused_computation | loop fusion | flops 32768 | bytes 263168 | tf_op jit(solution)/shard_map/jit(_where)/select_n | solution.py:439
  2.3 0.0 copy-start
  2.3 0.9 %copy-done = bf16[8,2,32,128]{3,2,1,0:T(8,128)(2,1)S(1)} copy-done((bf16[8,2,32,128]{3,2,1,0:T(8,128)(2,1)S(1)}, bf16[8,2,32,128]{3,2,1,0:T(8,128)(2,1)}, u32[]{:S(2)}) %copy-start) | copy-done | bytes 131096
  3.2 1.6 %front.1 = bf16[32,80,128]{2,1,0:T(8,128)(2,1)} custom-call(f32[8,32,128]{2,1,0:T(8,128)S(1)} %bitcast.2, bf16[8,2,32,128]{3,2,1,0:T(8,128)(2,1)S(1)} %copy-done), custom_call_target="tpu_custom_call" | custom-call | flops 1048576 | bytes 1048576 | tf_op jit(solution)/shard_map/front/pallas_call | solution.py:445
  4.8 8.5 %all-to-all-start = ((bf16[32,80,128]{2,1,0:T(8,128)(2,1)}), bf16[32,80,128]{2,1,0:T(8,128)(2,1)S(1)}, u32[]{:S(2)}, u32[]{:S(2)}) async-start(bf16[32,80,128]{2,1,0:T(8,128)(2,1)} %front.1), calls=%async_computation | async-start | bytes 1310720 | tf_op jit(solution)/shard_map/all_to_all | solution.py:417
  13.2 5.0 %collective-permute-start.1 = (f32[8,32,128]{2,1,0:T(8,128)S(1)}, f32[8,32,128]{2,1,0:T(8,128)S(1)}, u32[]{:S(2)}, u32[]{:S(2)}) collective-permute-start(f32[8,32,128]{2,1,0:T(8,128)S(1)} %bitcast.3), channel_id=1, source_target_pairs={{0,31},{1,2},{2,1},{3,4},{4,3},{5,6},{6,5},{7,8},{8,7},{9,10},{10,... | collective-permute-start | bytes 393224 | tf_op jit(solution)/shard_map/ppermute | solution.py:413
  18.3 0.0 collective-permute-start
  18.3 0.7 pad_add_fusion.meta
  19.0 0.0 copy-start.3
  19.0 0.0 copy-start.4
  19.0 8.9 %collective-permute-done.1.refs_2_ = f32[8,32,128]{2,1,0:T(8,128)S(1)} collective-permute-done((f32[8,32,128]{2,1,0:T(8,128)S(1)}, f32[8,32,128]{2,1,0:T(8,128)S(1)}, u32[]{:S(2)}, u32[]{:S(2)}) %collective-permute-start.1) | collective-permute-done | bytes 131104 | tf_op jit(solution)/shard_map/ppermute | solution.py:413
  27.9 0.0 collective-permute-done.refs_1_
  27.9 9.3 %near.2 = (f32[8,32,128]{2,1,0:T(8,128)S(1)}, bf16[8,128,1024]{2,1,0:T(8,128)(2,1)S(1)}) custom-call(s32[9,27]{1,0:T(8,128)S(1)} %pad_add_fusion.meta, f32[8,32,128]{2,1,0:T(8,128)S(1)} %bitcast.5, f32[8,32,128]{2,1,0:T(8,128)S(1)} %collective-permute-done.refs_1_, f32[8,32,128]{2,1,0:T(8,128)S(1)} %collective-permute-done.1.refs_2_, ...), custom_call_target="tpu_custom_call" | custom-call | flops 452984832 | bytes 14155776 | tf_op jit(solution)/shard_map/near/pallas_call | solution.py:475
  37.3 0.0 all-to-all-done.whole
  37.3 0.0 copy-done.1
  37.3 0.0 copy-done.2
  37.3 3.0 %image.1 = (f32[8,32,128]{2,1,0:T(8,128)S(1)}, bf16[8,32,128]{2,1,0:T(8,128)(2,1)S(1)}, bf16[16,80,128]{2,1,0:T(8,128)(2,1)S(1)}) custom-call(s32[8,32]{1,0:T(8,128)S(1)} %copy-done.3, s32[8]{0:T(128)S(1)} %copy-done.4, bf16[32,80,128]{2,1,0:T(8,128)(2,1)S(1)} %all-to-all-done.whole, bf16[8,128,1024]{2,1,0:T(8,128)(2,1)S(1)} %get-tuple-element.12.refs_0_, ...), custom_call_target="tpu_custom_call" | custom-call | tf_op jit(solution)/shard_map/image/pallas_call | solution.py:494
  40.3 12.0 %all_to_all.15.mine = bf16[16,80,128]{2,1,0:T(8,128)(2,1)S(1)} all-to-all(bf16[16,80,128]{2,1,0:T(8,128)(2,1)S(1)} %get-tuple-element.14), channel_id=1, replica_groups={{0,2,4,6,8,10,12,14,16,18,20,22,24,26,28,30},{1,3,5,7,9,11,13,15,17,19,..., dimensions={0} | all-to-all | bytes 655360 | tf_op jit(solution)/shard_map/all_to_all | solution.py:421
  52.3 0.0 collective-permute-start.2
  52.3 1.4 %collective-permute-start.4 = (bf16[8,32,128]{2,1,0:T(8,128)(2,1)S(1)}, bf16[8,32,128]{2,1,0:T(8,128)(2,1)S(1)}, u32[]{:S(2)}, u32[]{:S(2)}) collective-permute-start(bf16[8,32,128]{2,1,0:T(8,128)(2,1)S(1)} %get-tuple-element.15.refs_0_), channel_id=1, source_target_pairs={{0,31},{1,2},{2,1},{3,4},{4,3},{5,6},{6,5},{7,8},{8,7},{9,10},{10,... | collective-permute-start | bytes 196616 | tf_op jit(solution)/shard_map/ppermute | solution.py:413
  53.7 0.0 collective-permute-start.3
  53.7 5.6 %collective-permute-done.4.refs_2_ = bf16[8,32,128]{2,1,0:T(8,128)(2,1)S(1)} collective-permute-done((bf16[8,32,128]{2,1,0:T(8,128)(2,1)S(1)}, bf16[8,32,128]{2,1,0:T(8,128)(2,1)S(1)}, u32[]{:S(2)}, u32[]{:S(2)}) %collective-permute-start.4) | collective-permute-done | bytes 65568 | tf_op jit(solution)/shard_map/ppermute | solution.py:413
  59.3 0.0 collective-permute-done.3.refs_1_
  59.3 7.1 %near.3.refs_2_ = f32[8,32,128]{2,1,0:T(8,128)S(1)} custom-call(s32[9,27]{1,0:T(8,128)S(1)} %pad_add_fusion.meta, bf16[8,32,128]{2,1,0:T(8,128)(2,1)S(1)} %get-tuple-element.15.refs_0_, bf16[8,32,128]{2,1,0:T(8,128)(2,1)S(1)} %collective-permute-done.3.refs_1_, bf16[8,32,128]{2,1,0:T(8,128)(2,1)S(1)} %collective-permute-done.4.refs_2_, ...), custom_call_target="tpu_custom_call" | custom-call | flops 452984832 | bytes 14155776 | tf_op jit(solution)/shard_map/near/pallas_call | solution.py:475
  66.4 0.0 collective-permute-done.2.other
  66.4 3.6 %inner.1 = (f32[32,16,128]{2,1,0:T(8,128)}, f32[16,128]{1,0:T(8,128)S(1)}) custom-call(s32[8,32]{1,0:T(8,128)S(1)} %copy-done.3, s32[8]{0:T(128)S(1)} %copy-done.4, bf16[16,80,128]{2,1,0:T(8,128)(2,1)S(1)} %all_to_all.15.mine, bf16[16,80,128]{2,1,0:T(8,128)(2,1)S(1)} %collective-permute-done.2.other, bf16[8,128,1024]{2,1,0:T(8,128)(2,1)S(1)} %get-tuple-element.12.refs_0_, ...), custom_call_target="tpu_custom_call" | custom-call | tf_op jit(solution)/shard_map/inner/pallas_call | solution.py:510
  70.1 3.9 %all-to-all-start.2 = ((f32[32,16,128]{2,1,0:T(8,128)}), f32[32,16,128]{2,1,0:T(8,128)S(1)}, u32[]{:S(2)}, u32[]{:S(2)}) async-start(f32[32,16,128]{2,1,0:T(8,128)} %get-tuple-element.17), calls=%async_computation.2 | async-start | bytes 524288 | tf_op jit(solution)/shard_map/all_to_all | solution.py:417
  74.0 0.1 prepare.1
  74.1 8.8 %all-to-all-done.2.whole = f32[32,16,128]{2,1,0:T(8,128)S(1)} async-done(((f32[32,16,128]{2,1,0:T(8,128)}), f32[32,16,128]{2,1,0:T(8,128)S(1)}, u32[]{:S(2)}, u32[]{:S(2)}) %all-to-all-start.2) | async-done | bytes 262176 | tf_op jit(solution)/shard_map/all_to_all | solution.py:417
  82.9 0.0 copy-done.5
  82.9 1.5 %final.1 = (f32[8,2,16,128]{3,2,1,0:T(8,128)}, f32[2,16,16]{2,1,0:T(8,128)}, f32[4,16]{1,0:T(4,128)}) custom-call(f32[2]{0:T(128)S(1)} %copy-done.5, f32[32,16,128]{2,1,0:T(8,128)S(1)} %all-to-all-done.2.whole, f32[16,128]{1,0:T(8,128)S(1)} %get-tuple-element.18.head, f32[8,32,128]{2,1,0:T(8,128)S(1)} %get-tuple-element.19.first, ...), custom_call_target="tpu_custom_call" | custom-call | tf_op jit(solution)/shard_map/final/pallas_call | solution.py:531
  (5 shorter events, 0.0 us)
Async XLA Ops:
  2.3 0.9 %copy-start = (bf16[8,2,32,128]{3,2,1,0:T(8,128)(2,1)S(1)}, bf16[8,2,32,128]{3,2,1,0:T(8,128)(2,1)}, u32[]{:S(2)}) copy-start(bf16[8,2,32,128]{3,2,1,0:T(8,128)(2,1)} %refs_2_.1) | copy-start | bytes 393220
  4.8 32.5 %all-to-all-start = ((bf16[32,80,128]{2,1,0:T(8,128)(2,1)}), bf16[32,80,128]{2,1,0:T(8,128)(2,1)S(1)}, u32[]{:S(2)}, u32[]{:S(2)}) async-start(bf16[32,80,128]{2,1,0:T(8,128)(2,1)} %front.1), calls=%async_computation | async-start | bytes 1310720 | tf_op jit(solution)/shard_map/all_to_all | solution.py:417
  13.2 14.7 %collective-permute-start.1 = (f32[8,32,128]{2,1,0:T(8,128)S(1)}, f32[8,32,128]{2,1,0:T(8,128)S(1)}, u32[]{:S(2)}, u32[]{:S(2)}) collective-permute-start(f32[8,32,128]{2,1,0:T(8,128)S(1)} %bitcast.3), channel_id=1, source_target_pairs={{0,31},{1,2},{2,1},{3,4},{4,3},{5,6},{6,5},{7,8},{8,7},{9,10},{10,... | collective-permute-start | bytes 393224 | tf_op jit(solution)/shard_map/ppermute | solution.py:413
  18.3 9.7 %collective-permute-start = (f32[8,32,128]{2,1,0:T(8,128)S(1)}, f32[8,32,128]{2,1,0:T(8,128)S(1)}, u32[]{:S(2)}, u32[]{:S(2)}) collective-permute-start(f32[8,32,128]{2,1,0:T(8,128)S(1)} %bitcast.4), channel_id=1, source_target_pairs={{0,1},{1,0},{2,3},{3,2},{4,5},{5,4},{6,7},{7,6},{8,9},{9,8},{10,11... | collective-permute-start | bytes 393224 | tf_op jit(solution)/shard_map/ppermute | solution.py:413
  19.0 18.3 %copy-start.1 = (bf16[8,2,32,128]{3,2,1,0:T(8,128)(2,1)S(1)}, bf16[8,2,32,128]{3,2,1,0:T(8,128)(2,1)}, u32[]{:S(2)}) copy-start(bf16[8,2,32,128]{3,2,1,0:T(8,128)(2,1)} %refs_2_.1) | copy-start | bytes 393220
  19.0 18.3 %copy-start.2 = (bf16[8,2,32,128]{3,2,1,0:T(8,128)(2,1)S(1)}, bf16[8,2,32,128]{3,2,1,0:T(8,128)(2,1)}, u32[]{:S(2)}) copy-start(bf16[8,2,32,128]{3,2,1,0:T(8,128)(2,1)} %refs_1_.3) | copy-start | bytes 393220
  19.0 18.3 %copy-start.3 = (s32[8,32]{1,0:T(8,128)S(1)}, s32[8,32]{1,0:T(8,128)}, u32[]{:S(2)}) copy-start(s32[8,32]{1,0:T(8,128)} %far_list.3) | copy-start | bytes 3076
  19.0 18.3 %copy-start.4 = (s32[8]{0:T(128)S(1)}, s32[8]{0:T(128)}, u32[]{:S(2)}) copy-start(s32[8]{0:T(128)} %rows.3) | copy-start | bytes 100
  52.3 14.1 %collective-permute-start.2 = (bf16[16,80,128]{2,1,0:T(8,128)(2,1)S(1)}, bf16[16,80,128]{2,1,0:T(8,128)(2,1)S(1)}, u32[]{:S(2)}, u32[]{:S(2)}) collective-permute-start(bf16[16,80,128]{2,1,0:T(8,128)(2,1)S(1)} %all_to_all.15.mine), channel_id=1, source_target_pairs={{0,1},{1,0},{2,3},{3,2},{4,5},{5,4},{6,7},{7,6},{8,9},{9,8},{10,11... | collective-permute-start | bytes 983048 | tf_op jit(solution)/shard_map/ppermute | solution.py:413
  52.3 30.6 %copy-start.5 = (f32[2]{0:T(128)S(1)}, f32[2]{0:T(128)}, u32[]{:S(2)}) copy-start(f32[2]{0:T(128)} %weight.1) | copy-start | bytes 28
  52.3 7.0 %collective-permute-start.4 = (bf16[8,32,128]{2,1,0:T(8,128)(2,1)S(1)}, bf16[8,32,128]{2,1,0:T(8,128)(2,1)S(1)}, u32[]{:S(2)}, u32[]{:S(2)}) collective-permute-start(bf16[8,32,128]{2,1,0:T(8,128)(2,1)S(1)} %get-tuple-element.15.refs_0_), channel_id=1, source_target_pairs={{0,31},{1,2},{2,1},{3,4},{4,3},{5,6},{6,5},{7,8},{8,7},{9,10},{10,... | collective-permute-start | bytes 196616 | tf_op jit(solution)/shard_map/ppermute | solution.py:413
  53.7 5.6 %collective-permute-start.3 = (bf16[8,32,128]{2,1,0:T(8,128)(2,1)S(1)}, bf16[8,32,128]{2,1,0:T(8,128)(2,1)S(1)}, u32[]{:S(2)}, u32[]{:S(2)}) collective-permute-start(bf16[8,32,128]{2,1,0:T(8,128)(2,1)S(1)} %get-tuple-element.15.refs_0_), channel_id=1, source_target_pairs={{0,1},{1,0},{2,3},{3,2},{4,5},{5,4},{6,7},{7,6},{8,9},{9,8},{10,11... | collective-permute-start | bytes 196616 | tf_op jit(solution)/shard_map/ppermute | solution.py:413
  70.1 12.8 %all-to-all-start.2 = ((f32[32,16,128]{2,1,0:T(8,128)}), f32[32,16,128]{2,1,0:T(8,128)S(1)}, u32[]{:S(2)}, u32[]{:S(2)}) async-start(f32[32,16,128]{2,1,0:T(8,128)} %get-tuple-element.17), calls=%async_computation.2 | async-start | bytes 524288 | tf_op jit(solution)/shard_map/all_to_all | solution.py:417
